TPU v7x, 128 devices: a whole 4x4x4 slice. The times are simulated.
128 devices in a mesh: narrow: 4 (over y_hi, core), wide: 32 (over z, y_lo, x).
Axes of the slice: x: 4, y: 4 (y_hi: 2, y_lo: 2; y = y_hi * 2 + y_lo), z: 4, core: 2. Of those that a mesh axis runs over, the one named last changes fastest.
Arguments:
- residual: float32 [16, 2048, 2048], P(None, 'wide', 'narrow'), may hold values from -6 to 6
- counts: int32 [16, 2048, 2048], P(None, 'wide', 'narrow'), may hold values from 0 to 4
- screening: float32 [16], replicated, may hold values from 0.02 to 0.5
- even_y: float32 [1024, 1024], replicated, may hold values from -0.1875 to 0.1875
- odd_y: float32 [1024, 1024], replicated, may hold values from -0.1875 to 0.1875
- even_z: float32 [1024, 1024], replicated, may hold values from -0.1875 to 0.1875
- odd_z: float32 [1024, 1024], replicated, may hold values from -0.1875 to 0.1875
- lam_y: float32 [2048], replicated, may hold values from 0.05 to 4
- lam_z: float32 [2048], replicated, may hold values from 0.05 to 4
Outputs:
- correction: float32 [16, 2048, 2048], P(None, 'wide', 'narrow')
All inputs are finite; a program needn't handle non-finite values.
Results may differ from a plain program's by a relative error of at most 0.000071.
Values sent between devices are 32-bit elements; how exact they have to be, the bound alone decides.
No kernel may reach another device: no remote copies, remote signals or barrier semaphores. Data moves between devices by JAX's collectives and lax.ppermute only.
A program may use at most 192 MiB of HBM per device.

v0:
```python
import jax
import jax.numpy as jnp
from jax import lax
from jax.sharding import PartitionSpec as P


def product(form, left, right):
    return jnp.einsum(
        form, left, right, preferred_element_type=jnp.float32, precision=lax.Precision.HIGHEST
    )


def forward_rows(even_y, odd_y, pieces):
    half_y = pieces.shape[2] // 2
    flipped = pieces[:, :, ::-1]
    first = pieces[:, :, :half_y]
    return jnp.concatenate(
        [
            product("pzy,yk->zpk", first + flipped[:, :, :half_y], even_y),
            product("pzy,yk->zpk", first - flipped[:, :, :half_y], odd_y),
        ],
        2,
    )


def regroup(values, first, second):
    length = values.shape[0]
    rest = values.shape[1:]
    inner = length // (first * second)
    shaped = values.reshape((first, second, inner) + rest)
    order = (1, 0) + tuple(range(2, len(rest) + 3))
    return jnp.transpose(shaped, order).reshape((length,) + rest)


def on_device(residual, counts, screening, even_y, odd_y, even_z, odd_z, lam_y, lam_z):
    narrow_count = lax.axis_size("narrow")
    wide_count = lax.axis_size("wide")
    planes = residual.shape[0]
    source = residual + 0.3 * (counts.astype(jnp.float32) - 2.0)
    yfolded = forward_rows(
        even_y, odd_y, lax.all_to_all(source, "narrow", split_axis=1, concat_axis=2, tiled=True)
    )
    zlocal, _, full_modes = yfolded.shape
    mode_count = full_modes // (narrow_count * wide_count)
    mixed = lax.all_to_all(yfolded, ("narrow", "wide"), split_axis=2, concat_axis=0, tiled=True)
    zfull = regroup(mixed, narrow_count, wide_count)
    length = zfull.shape[0]
    half_z = length // 2
    columns = zfull.reshape(length, planes * mode_count)
    group = lax.axis_index("narrow") * wide_count + lax.axis_index("wide")
    lam_local = lax.dynamic_slice_in_dim(lam_y, group * mode_count, mode_count)
    flipped = columns[::-1]
    first = columns[:half_z]
    spectral = jnp.concatenate(
        [
            product("zm,zc->mc", even_z, first + flipped[:half_z]),
            product("zm,zc->mc", odd_z, first - flipped[:half_z]),
        ],
        0,
    )
    shift = (lam_local[None, :] + screening[:, None]).reshape(1, planes * mode_count)
    scaled = spectral / (lam_z[:, None] + shift)
    zeven = product("zm,mc->zc", even_z, scaled[:half_z])
    zodd = product("zm,mc->zc", odd_z, scaled[half_z:])
    back = jnp.concatenate([zeven + zodd, (zeven - zodd)[::-1]], 0)
    outgoing = regroup(back, wide_count, narrow_count)
    yback = lax.all_to_all(
        outgoing.reshape(length, planes, mode_count),
        ("narrow", "wide"),
        split_axis=0,
        concat_axis=2,
        tiled=True,
    )
    half_y = full_modes // 2
    yeven = product("zpk,yk->pzy", yback[:, :, :half_y], even_y)
    yodd = product("zpk,yk->pzy", yback[:, :, half_y:], odd_y)
    rows_done = jnp.concatenate([yeven + yodd, (yeven - yodd)[:, :, ::-1]], 2)
    return lax.all_to_all(rows_done, "narrow", split_axis=2, concat_axis=1, tiled=True)


def solution(mesh):
    in_specs = (
        P(None, "wide", "narrow"),
        P(None, "wide", "narrow"),
        P(),
        P(),
        P(),
        P(),
        P(),
        P(),
        P(),
    )
    out_specs = P(None, "wide", "narrow")
    return jax.shard_map(
        on_device, mesh=mesh, in_specs=in_specs, out_specs=out_specs, check_vma=False
    )
```

profile of v0, /device:TPU:1, one launch (start us, length us, event | category | flops | bytes accessed | tf_op | source)
XLA Modules:
  0.0 407.5 jit_solution(10091726912696891183)
XLA Ops:
  4.8 32.4 %all_to_all.69 = f32[16,64,512]{2,0,1:T(8,128)S(1)} all-to-all(f32[16,64,512]{2,0,1:T(8,128)S(1)} %copy_add_fusion), channel_id=1, replica_groups=mesh['narrow'=4,'wide'=32] {'narrow'}, dimensions={1} | all-to-all | bytes 4194304 | tf_op jit(solution)/shard_map/all_to_all | solution.py:41
  57.6 11.1 %copy.23 = f32[16,16,2048]{0,1,2:T(8,128)} copy(f32[16,16,2048]{2,0,1:T(8,128)S(1)} %pad_maximum_fusion) | data formatting | bytes 4194304 | tf_op jit(solution)/shard_map/concatenate | solution.py:17
  68.6 12.3 %reshape.31 = f32[128,1,4096]{2,1,0:T(1,128)} reshape(f32[2048,16,16]{2,1,0:T(8,128)} %bitcast.68) | data formatting | bytes 4194304
  81.0 8.8 %all-to-all-start.1 = ((f32[128,1,4096]{2,1,0:T(1,128)}), f32[128,1,4096]{2,1,0:T(1,128)S(1)}, u32[]{:S(2)}, u32[]{:S(2)}) async-start(f32[128,1,4096]{2,1,0:T(1,128)} %reshape.31), calls=%async_computation.1 | async-start | bytes 4194304 | tf_op jit(solution)/shard_map/all_to_all | solution.py:45
  90.7 29.3 %all-to-all-done.1 = f32[128,1,4096]{2,1,0:T(1,128)S(1)} async-done(((f32[128,1,4096]{2,1,0:T(1,128)}), f32[128,1,4096]{2,1,0:T(1,128)S(1)}, u32[]{:S(2)}, u32[]{:S(2)}) %all-to-all-start.1) | async-done | bytes 2097184 | tf_op jit(solution)/shard_map/all_to_all | solution.py:45
  121.8 7.2 %reduce = f32[128,4096]{1,0:T(8,128)S(1)} reduce(f32[128,1,4096]{2,1,0:T(1,128)} %copy-done.4, f32[]{:T(128)} %broadcast.12), dimensions={1}, to_apply=%all_to_all.54.reduce_sub_computation | reduce | bytes 4194308 | tf_op jit(solution)/shard_map/all_to_all | solution.py:45
  129.0 8.9 %reshape.32 = f32[2048,16,16]{2,1,0:T(8,128)} reshape(f32[128,4096]{1,0:T(8,128)S(1)} %reduce) | data formatting | bytes 4194304
  138.0 18.8 %copy.25 = f32[4,32,16,16,16]{4,3,2,0,1:T(8,128)} copy(f32[4,32,16,16,16]{2,3,4,1,0:T(8,128)} %bitcast.72) | data formatting | bytes 4194304 | tf_op jit(solution)/shard_map/reshape | solution.py:30
  156.7 11.0 %fusion.28 = (f32[16,4,16,16,16]{4,3,2,1,0:T(8,128)}, f32[16,4,16,16,16]{4,3,2,1,0:T(8,128)}) fusion(f32[32,4,16,16,16]{4,3,2,1,0:T(8,128)} %bitcast.71), kind=kLoop, calls=%fused_computation.37 | loop fusion | bytes 4194304 | tf_op jit(solution)/shard_map/slice | solution.py:56
  174.3 6.1 %slice.42 = f32[1024,256]{1,0:T(8,128)S(1)} reshape(f32[16,4,16,16,16]{4,3,2,1,0:T(8,128)} %get-tuple-element.6) | data formatting | bytes 2097152 | tf_op jit(solution)/shard_map/slice | solution.py:53
  180.4 6.3 %convolution_bitcast_fusion.1 = f32[1024,256]{0,1:T(8,128)S(1)} fusion(f32[1024,1024]{1,0:T(8,128)} %param.14, f32[1024,256]{1,0:T(8,128)S(1)} %slice.42, f32[1024,256]{1,0:T(8,128)S(1)} %slice.45), kind=kOutput, calls=%fused_computation.19 | convolution fusion | flops 3221487616 | bytes 7340032 | tf_op jit(solution)/shard_map/zm,zc->mc/dot_general | solution.py:8
  205.8 8.7 %reshape_reshape.4 = f32[2048,16,16]{2,1,0:T(8,128)} reshape(f32[4,32,16,256]{3,2,1,0:T(8,128)S(1)} %copy.27) | data formatting | bytes 4194304 | tf_op jit(solution)/shard_map/reshape;reshape | solution.py:68
  214.5 11.4 %reshape.33 = f32[128,1,4096]{2,1,0:T(1,128)S(1)} reshape(f32[2048,16,16]{2,1,0:T(8,128)} %reshape_reshape.4) | data formatting | bytes 4194304
  225.9 35.1 %all_to_all.70 = f32[128,1,4096]{2,1,0:T(1,128)} all-to-all(f32[128,1,4096]{2,1,0:T(1,128)S(1)} %reshape.33), channel_id=1, replica_groups=mesh['narrow'=4,'wide'=32] {'narrow','wide'}, dimensions={0} | all-to-all | bytes 4194304 | tf_op jit(solution)/shard_map/all_to_all | solution.py:67
  260.9 7.2 %reduce.1 = f32[128,4096]{1,0:T(8,128)S(1)} reduce(f32[128,1,4096]{2,1,0:T(1,128)} %all_to_all.70, f32[]{:T(128)} %broadcast.12), dimensions={1}, to_apply=%all_to_all.57.reduce_sub_computation | reduce | bytes 4194308 | tf_op jit(solution)/shard_map/all_to_all | solution.py:67
  268.2 8.9 %reshape.34 = f32[2048,16,16]{2,1,0:T(8,128)} reshape(f32[128,4096]{1,0:T(8,128)S(1)} %reduce.1) | data formatting | bytes 4194304
  277.1 17.7 %copy.29 = f32[16,16,128,16]{3,2,1,0:T(8,128)} copy(f32[16,16,128,16]{3,1,0,2:T(8,128)} %bitcast.73) | data formatting | bytes 4194304 | tf_op jit(solution)/shard_map/all_to_all | solution.py:67
  294.8 14.2 %all_to_all.60 = f32[16,16,2048]{2,1,0:T(8,128)S(1)} reshape(f32[16,16,128,16]{3,2,1,0:T(8,128)} %copy.29) | data formatting | bytes 4194304 | tf_op jit(solution)/shard_map/all_to_all | solution.py:67
  325.8 11.1 %copy.30 = f32[16,16,2048]{0,1,2:T(8,128)} copy(f32[16,16,2048]{2,0,1:T(8,128)S(1)} %pad_maximum_fusion.2) | data formatting | bytes 4194304 | tf_op jit(solution)/shard_map/concatenate | solution.py:77
  336.8 9.1 %reshape.35 = f32[4,1,131072]{2,1,0:T(1,128)S(1)} reshape(f32[2048,16,16]{2,1,0:T(8,128)} %bitcast.69) | data formatting | bytes 4194304
  345.9 30.8 %all_to_all.71 = f32[4,1,131072]{2,1,0:T(1,128)} all-to-all(f32[4,1,131072]{2,1,0:T(1,128)S(1)} %reshape.35), channel_id=1, replica_groups=mesh['narrow'=4,'wide'=32] {'narrow'}, dimensions={0} | all-to-all | bytes 4194304 | tf_op jit(solution)/shard_map/all_to_all | solution.py:78
  376.7 7.6 %reduce.2 = f32[4,131072]{1,0:T(4,128)S(1)} reduce(f32[4,1,131072]{2,1,0:T(1,128)} %all_to_all.71, f32[]{:T(128)} %broadcast.12), dimensions={1}, to_apply=%all_to_all.61.reduce_sub_computation | reduce | bytes 4194308 | tf_op jit(solution)/shard_map/all_to_all | solution.py:78
  384.4 11.5 %reshape.36 = f32[2048,16,16]{2,1,0:T(8,128)} reshape(f32[4,131072]{1,0:T(4,128)S(1)} %reduce.2) | data formatting | bytes 4194304
  395.9 11.1 %copy.31 = f32[16,4,16,512]{3,2,1,0:T(8,128)} copy(f32[16,4,16,512]{0,2,3,1:T(8,128)} %bitcast.70) | data formatting | bytes 4194304 | tf_op jit(solution)/shard_map/all_to_all | solution.py:78
  (40 shorter events, 70.2 us)
Async XLA Ops:
  47.8 5.9 %copy-start.1 = (f32[1024,1024]{1,0:T(8,128)S(1)}, f32[1024,1024]{1,0:T(8,128)}, u32[]{:S(2)}) copy-start(f32[1024,1024]{1,0:T(8,128)} %param.13) | copy-start | bytes 12582916
  81.0 9.6 %copy-start.6 = (f32[16]{0:T(128)S(1)}, f32[16]{0:T(128)}, u32[]{:S(2)}) copy-start(f32[16]{0:T(128)} %param.11) | copy-start | bytes 196
  81.0 39.0 %all-to-all-start.1 = ((f32[128,1,4096]{2,1,0:T(1,128)}), f32[128,1,4096]{2,1,0:T(1,128)S(1)}, u32[]{:S(2)}, u32[]{:S(2)}) async-start(f32[128,1,4096]{2,1,0:T(1,128)} %reshape.31), calls=%async_computation.1 | async-start | bytes 4194304 | tf_op jit(solution)/shard_map/all_to_all | solution.py:45
  120.0 1.3 copy-start.4
  180.4 6.3 %copy-start = (f32[1024,1024]{1,0:T(8,128)S(1)}, f32[1024,1024]{1,0:T(8,128)}, u32[]{:S(2)}) copy-start(f32[1024,1024]{1,0:T(8,128)} %param.15) | copy-start | bytes 12582916
  186.7 3.6 copy-start.5
  190.7 3.8 copy-start.2
  309.0 6.1 %copy-start.3 = (f32[1024,1024]{1,0:T(8,128)S(1)}, f32[1024,1024]{1,0:T(8,128)}, u32[]{:S(2)}) copy-start(f32[1024,1024]{1,0:T(8,128)} %param.12) | copy-start | bytes 12582916
where the time goes:
time: 412 us; the launch traced here: 407 us
  local copies, waits for them, and re-layouts  201 us (49%)
  blocking collectives  98.3 us (24%)
  matrix products  39.2 us (10%)
  other arithmetic  30.2 us (7%)
  waiting for transfers between devices  29.3 us (7%)
  starting transfers between devices  8.8 us (2%)
    unnamed x20, local copies, waits for them, and re-layouts  63.5 us
    dot_general x8, matrix products, product(): jnp.einsum(form, left, right, preferred_element_type=jnp.float32, precisi...  39.2 us
    all_to_all x1, blocking collectives, on_device(): lax.all_to_all(outgoing.reshape(length, planes, mode_count), ('narrow', '...  35.1 us
    all_to_all x1, blocking collectives, on_device(): lax.all_to_all(source, 'narrow', split_axis=1, concat_axis=2, tiled=True)  32.4 us
    all_to_all x2, local copies, waits for them, and re-layouts, on_device(): lax.all_to_all(outgoing.reshape(length, planes, mode_count), ('narrow', '...  31.9 us
    all_to_all x1, blocking collectives, on_device(): lax.all_to_all(rows_done, 'narrow', split_axis=2, concat_axis=1, tiled=True)  30.8 us
    all_to_all x1, waiting for transfers between devices, on_device(): lax.all_to_all(yfolded, ('narrow', 'wide'), split_axis=2, concat_axis=0,...  29.3 us
    reshape x1, local copies, waits for them, and re-layouts, regroup(): shaped = values.reshape((first, second, inner) + rest)  18.8 us
  transfers between devices with their start and end apart: 1, of which 1 were waited for; matrix products, arithmetic and copies ran while one was open for 0% of the time, Pallas kernels for 0%

commit v1 on v0

v1 whole, which is shorter than its diff:
```python
import jax
import jax.numpy as jnp
from jax import lax
from jax.experimental import pallas as pl
from jax.experimental.pallas import tpu as pltpu
from jax.sharding import Mesh, PartitionSpec as P

F32 = jnp.float32
BF16 = jnp.bfloat16
ROWS = 256
TILE = 256
HALF = 1024
GATHER_Y = ("yh", "z", "yl", "core")
GATHER_Z = ("x", "core")
VMEM = pl.BlockSpec(memory_space=pltpu.VMEM)
NN = (((1,), (0,)), ((), ()))
NT = (((1,), (1,)), ((), ()))
TN = (((0,), (0,)), ((), ()))


def split(value):
    high = value.astype(BF16)
    low = (value - high.astype(F32)).astype(BF16)
    return high, low


def dot(left, right, dims):
    return lax.dot_general(left, right, dims, preferred_element_type=F32)


def product(left, right, dims):
    return (
        dot(left[0], right[0], dims)
        + dot(left[0], right[1], dims)
        + dot(left[1], right[0], dims)
    )


def mirror():
    row = lax.broadcasted_iota(jnp.int32, (TILE, TILE), 0)
    column = lax.broadcasted_iota(jnp.int32, (TILE, TILE), 1)
    return jnp.where(row + column == TILE - 1, 1.0, 0.0).astype(BF16)


def flip_lanes(value, flipper):
    high, low = split(value)
    return dot(high, flipper, NN) + dot(low, flipper, NN)


def flip_rows(value, flipper):
    high, low = split(value)
    return dot(flipper, high, NN) + dot(flipper, low, NN)


def split_kernel(matrix_ref, high_ref, low_ref):
    high_ref[...], low_ref[...] = split(matrix_ref[...])


def split_matrix(matrix):
    block = pl.BlockSpec((256, HALF), lambda i: (i, 0))
    return pl.pallas_call(
        split_kernel,
        grid=(HALF // 256,),
        in_specs=[block],
        out_specs=[block, block],
        out_shape=[jax.ShapeDtypeStruct((HALF, HALF), BF16)] * 2,
        name="split_matrix",
    )(matrix)


def forward_y_kernel(x_ref, eh_ref, el_ref, oh_ref, ol_ref, out_ref):
    flipper = mirror()
    sym, anti = [], []
    for core in range(2):
        for part in range(2):
            lanes = slice(part * TILE, (part + 1) * TILE)
            other = slice((1 - part) * TILE, (2 - part) * TILE)
            low = x_ref[0, :, core, :, lanes].reshape(ROWS, TILE)
            high = x_ref[1, :, 1 - core, :, other].reshape(ROWS, TILE)
            high = flip_lanes(high, flipper)
            sym.append(split(low + high))
            anti.append(split(low - high))
    for base, sides, h_ref, l_ref in ((0, sym, eh_ref, el_ref), (4, anti, oh_ref, ol_ref)):
        left = tuple(jnp.concatenate([s[i] for s in sides], 1) for i in range(2))
        for block in range(4):
            lanes = slice(block * TILE, (block + 1) * TILE)
            out_ref[base + block] = product(left, (h_ref[:, lanes], l_ref[:, lanes]), NN)


def forward_y(x, even, odd):
    return pl.pallas_call(
        forward_y_kernel,
        in_specs=[VMEM] * 5,
        out_specs=VMEM,
        out_shape=jax.ShapeDtypeStruct((8, ROWS, TILE), F32),
        compiler_params=pltpu.CompilerParams(vmem_limit_bytes=48 << 20),
        name="forward_y",
    )(x.reshape(2, 8, 2, 32, 512), *even, *odd)


def solve_z_kernel(x_ref, eh_ref, el_ref, oh_ref, ol_ref, lam_ref, shift_ref, out_ref):
    flipper = mirror()
    sym, anti = [], []
    for t in range(4):
        low = x_ref[:, t].reshape(TILE, TILE)
        high = flip_rows(x_ref[:, 7 - t].reshape(TILE, TILE), flipper)
        sym.append(split(low + high))
        anti.append(split(low - high))
    results = []
    for parity, sides, h_ref, l_ref in ((0, sym, eh_ref, el_ref), (1, anti, oh_ref, ol_ref)):
        right = tuple(jnp.concatenate([s[i] for s in sides], 0) for i in range(2))
        matrix = (h_ref[...], l_ref[...])
        spectral = product(matrix, right, TN)
        scaled = spectral / (lam_ref[parity] + shift_ref[...])
        results.append(product(matrix, split(scaled), NN))
    total = results[0] + results[1]
    rest = results[0] - results[1]
    for t in range(4):
        rows = slice(t * TILE, (t + 1) * TILE)
        out_ref[:, t] = total[rows].reshape(8, 32, TILE)
        out_ref[:, 7 - t] = flip_rows(rest[rows], flipper).reshape(8, 32, TILE)


def solve_z(x, even, odd, lam, shift):
    return pl.pallas_call(
        solve_z_kernel,
        in_specs=[VMEM] * 7,
        out_specs=VMEM,
        out_shape=jax.ShapeDtypeStruct((8, 8, 32, TILE), F32),
        compiler_params=pltpu.CompilerParams(vmem_limit_bytes=48 << 20),
        name="solve_z",
    )(x.reshape(8, 8, 32, TILE), *even, *odd, lam, shift)


def backward_y_kernel(x_ref, eh_ref, el_ref, oh_ref, ol_ref, out_ref):
    flipper = mirror()
    even = split(jnp.concatenate([x_ref[i] for i in range(4)], 1))
    odd = split(jnp.concatenate([x_ref[i] for i in range(4, 8)], 1))
    for block in range(4):
        core, part = divmod(block, 2)
        rows = slice(block * TILE, (block + 1) * TILE)
        yeven = product(even, (eh_ref[rows], el_ref[rows]), NT)
        yodd = product(odd, (oh_ref[rows], ol_ref[rows]), NT)
        lanes = slice(part * TILE, (part + 1) * TILE)
        other = slice((1 - part) * TILE, (2 - part) * TILE)
        out_ref[0, :, core, :, lanes] = (yeven + yodd).reshape(8, 32, TILE)
        flipped = flip_lanes(yeven - yodd, flipper)
        out_ref[1, :, 1 - core, :, other] = flipped.reshape(8, 32, TILE)


def backward_y(x, even, odd):
    return pl.pallas_call(
        backward_y_kernel,
        in_specs=[VMEM] * 5,
        out_specs=VMEM,
        out_shape=jax.ShapeDtypeStruct((2, 8, 2, 32, 512), F32),
        compiler_params=pltpu.CompilerParams(vmem_limit_bytes=48 << 20),
        name="backward_y",
    )(x, *even, *odd)


def on_device(residual, counts, screening, even_y, odd_y, even_z, odd_z, lam_y, lam_z):
    plane = (lax.axis_index("yh") * 4 + lax.axis_index("z")) * 2 + lax.axis_index("yl")
    modes = lax.axis_index("x") * 2 + lax.axis_index("core")
    source = residual + 0.3 * (counts.astype(F32) - 2.0)
    gathered = lax.all_to_all(source.reshape(32, 32, 512), GATHER_Y, 0, 0, tiled=True)
    ey, oy, ez, oz = (split_matrix(m) for m in (even_y, odd_y, even_z, odd_z))
    shift = lax.dynamic_slice_in_dim(lam_y, modes * TILE, TILE)
    shift = (shift + lax.dynamic_slice_in_dim(screening, plane, 1)).reshape(1, TILE)
    lam = lam_z.reshape(2, HALF, 1)
    along = forward_y(gathered, ey, oy)
    columns = lax.all_to_all(along, GATHER_Z, 0, 0, tiled=True)
    back = solve_z(columns, ez, oz, lam, shift)
    rows = lax.all_to_all(back.reshape(8, ROWS, TILE), GATHER_Z, 0, 0, tiled=True)
    done = backward_y(rows, ey, oy)
    done = lax.all_to_all(done.reshape(32, 32, 512), GATHER_Y, 0, 0, tiled=True)
    return done.reshape(16, 64, 512)


def solution(mesh):
    fine = Mesh(mesh.devices.reshape(2, 2, 4, 2, 4), ("yh", "core", "z", "yl", "x"))
    split_spec = P(None, ("z", "yl", "x"), ("yh", "core"))
    return jax.shard_map(
        on_device,
        mesh=fine,
        in_specs=(split_spec, split_spec) + (P(),) * 7,
        out_specs=split_spec,
        check_vma=False,
    )
```

time: 412 us -> 168 us (0.41)
  local copies, waits for them, and re-layouts: 201 us -> 4.15 us
  Pallas kernels: 0 us -> 47.7 us
  matrix products: 39.2 us -> 0 us
  blocking collectives: 98.3 us -> 63.3 us
  other arithmetic: 30.2 us -> 5.44 us
  starting transfers between devices: 8.8 us -> 14.1 us
    unnamed x20 -> x7, local copies, waits for them, and re-layouts: 63.5 us -> 2.64 us
    all_to_all x6 -> x0, local copies, waits for them, and re-layouts: 48.9 us -> none  [the longest x2 31.9 us: on_device(): lax.all_to_all(outgoing.reshape(length, planes, mode_count), ('narrow', '...]
    pallas_call x0 -> x7, Pallas kernels: none -> 47.7 us  [the longest x4 19 us: split_matrix(): pl.pallas_call(split_kernel, grid=(HALF // 256,), in_specs=[block], out_s...]
    dot_general x8 -> x0, matrix products: 39.2 us -> none  [product(): jnp.einsum(form, left, right, preferred_element_type=jnp.float32, precisi...]
    all_to_all x3 -> x2, blocking collectives: 98.3 us -> 63.3 us  [the longest x1 33.6 us: on_device(): done = lax.all_to_all(done.reshape(32, 32, 512), GATHER_Y, 0, 0, tiled=True)]
    slice x6 -> x0, local copies, waits for them, and re-layouts: 28.8 us -> none  [the longest x3 17.5 us: on_device(): flipped[:half_z]]
    concatenate x3 -> x0, local copies, waits for them, and re-layouts: 23.9 us -> none  [the longest x1 11.1 us: forward_rows(): jnp.concatenate([product('pzy,yk->zpk', first + flipped[:, :, :half_y], e...]
    all_to_all x3 -> x0, other arithmetic: 22.1 us -> none  [the longest x1 7.63 us: on_device(): lax.all_to_all(rows_done, 'narrow', split_axis=2, concat_axis=1, tiled=True)]
  transfers between devices with their start and end apart: 1 -> 2, of which waited for: 1 -> 2; matrix products, arithmetic and copies ran while one was open for 0% -> 2% of each run, Pallas kernels for 0% -> 11%
where the time goes in v1:
time: 168 us; the launch traced here: 167 us
  blocking collectives  63.3 us (38%)
  Pallas kernels  47.7 us (28%)
  waiting for transfers between devices  32.6 us (19%)
  starting transfers between devices  14.1 us (8%)
  other arithmetic  5.44 us (3%)
  local copies, waits for them, and re-layouts  4.15 us (2%)
    all_to_all x1, blocking collectives, on_device(): done = lax.all_to_all(done.reshape(32, 32, 512), GATHER_Y, 0, 0, tiled=True)  33.6 us
    all_to_all x1, blocking collectives, on_device(): lax.all_to_all(back.reshape(8, ROWS, TILE), GATHER_Z, 0, 0, tiled=True)  29.8 us
    pallas_call x4, Pallas kernels, split_matrix(): pl.pallas_call(split_kernel, grid=(HALF // 256,), in_specs=[block], out_s...  19 us
    all_to_all x1, waiting for transfers between devices, on_device(): lax.all_to_all(source.reshape(32, 32, 512), GATHER_Y, 0, 0, tiled=True)  18.6 us
    all_to_all x1, waiting for transfers between devices, on_device(): columns = lax.all_to_all(along, GATHER_Z, 0, 0, tiled=True)  14 us
    pallas_call x1, Pallas kernels, solve_z(): pl.pallas_call(solve_z_kernel, in_specs=[VMEM] * 7, out_specs=VMEM, out_s...  13.8 us
    all_to_all x1, starting transfers between devices, on_device(): lax.all_to_all(source.reshape(32, 32, 512), GATHER_Y, 0, 0, tiled=True)  9.6 us
    pallas_call x1, Pallas kernels, backward_y(): pl.pallas_call(backward_y_kernel, in_specs=[VMEM] * 5, out_specs=VMEM, ou...  7.7 us
  transfers between devices with their start and end apart: 2, of which 2 were waited for; matrix products, arithmetic and copies ran while one was open for 2% of the time, Pallas kernels for 11%

profile of v1, /device:TPU:1, one launch (start us, length us, event | category | flops | bytes accessed | tf_op | source)
XLA Modules:
  0.0 167.4 jit_solution(7566129735212772357)
XLA Ops:
  0.0 4.1 %multiply_add_fusion = f32[16,64,512]{2,1,0:T(8,128)} fusion(f32[16,64,512]{2,1,0:T(8,128)} %param.9, s32[16,64,512]{2,1,0:T(8,128)} %param.10), kind=kLoop, calls=%fused_computation | loop fusion | flops 2097152 | bytes 6291456 | tf_op jit(solution)/shard_map/add | solution.py:165
  4.1 9.6 %all-to-all-start = ((f32[32,32,512]{2,1,0:T(8,128)}), f32[32,32,512]{2,1,0:T(8,128)S(1)}, u32[]{:S(2)}, u32[]{:S(2)}) async-start(f32[32,32,512]{2,1,0:T(8,128)} %bitcast.13), calls=%async_computation | async-start | bytes 4194304 | tf_op jit(solution)/shard_map/all_to_all | solution.py:166
  13.7 4.7 %split_matrix.4 = (bf16[1024,1024]{1,0:T(8,128)(2,1)}, bf16[1024,1024]{1,0:T(8,128)(2,1)}) custom-call(f32[1024,1024]{1,0:T(8,128)} %matrix_ref.4), custom_call_target="tpu_custom_call" | custom-call | tf_op jit(solution)/shard_map/split_matrix/pallas_call | solution.py:61
  18.4 4.8 %split_matrix.5 = (bf16[1024,1024]{1,0:T(8,128)(2,1)}, bf16[1024,1024]{1,0:T(8,128)(2,1)}) custom-call(f32[1024,1024]{1,0:T(8,128)} %matrix_ref.5), custom_call_target="tpu_custom_call" | custom-call | tf_op jit(solution)/shard_map/split_matrix/pallas_call | solution.py:61
  23.2 18.6 %all-to-all-done = f32[32,32,512]{2,1,0:T(8,128)S(1)} async-done(((f32[32,32,512]{2,1,0:T(8,128)}), f32[32,32,512]{2,1,0:T(8,128)S(1)}, u32[]{:S(2)}, u32[]{:S(2)}) %all-to-all-start) | async-done | bytes 2097184 | tf_op jit(solution)/shard_map/all_to_all | solution.py:166
  41.8 7.2 %forward_y.1 = f32[8,256,256]{2,1,0:T(8,128)S(1)} custom-call(f32[2,8,2,32,512]{4,3,2,1,0:T(8,128)S(1)} %bitcast.9, bf16[1024,1024]{1,0:T(8,128)(2,1)} %get-tuple-element.13.eh_ref, bf16[1024,1024]{1,0:T(8,128)(2,1)} %get-tuple-element.14.el_ref, bf16[1024,1024]{1,0:T(8,128)(2,1)} %get-tuple-element.15.oh_ref, bf16[1024,1024]{1,0:T(8,128)(2,1)} %get-tuple-element.16.ol_ref), custom_call_target="tpu_custom_call" | custom-call | tf_op jit(solution)/shard_map/forward_y/pallas_call | solution.py:91
  49.0 0.0 copy-start
  49.0 1.3 copy-done
  50.3 0.0 copy-start.1
  50.3 4.5 %all-to-all-start.1 = ((f32[8,256,256]{2,1,0:T(8,128)}), f32[8,256,256]{2,1,0:T(8,128)S(1)}, u32[]{:S(2)}, u32[]{:S(2)}) async-start(f32[8,256,256]{2,1,0:T(8,128)} %copy-done), calls=%async_computation.1 | async-start | bytes 4194304 | tf_op jit(solution)/shard_map/all_to_all | solution.py:172
  54.8 0.0 copy-done.1
  54.8 0.9 reshape.32.lam_ref
  55.7 4.7 %split_matrix.6 = (bf16[1024,1024]{1,0:T(8,128)(2,1)}, bf16[1024,1024]{1,0:T(8,128)(2,1)}) custom-call(f32[1024,1024]{1,0:T(8,128)} %matrix_ref.6), custom_call_target="tpu_custom_call" | custom-call | tf_op jit(solution)/shard_map/split_matrix/pallas_call | solution.py:61
  60.5 0.0 copy-start.2
  60.5 4.7 %split_matrix.7 = (bf16[1024,1024]{1,0:T(8,128)(2,1)}, bf16[1024,1024]{1,0:T(8,128)(2,1)}) custom-call(f32[1024,1024]{1,0:T(8,128)} %matrix_ref.7), custom_call_target="tpu_custom_call" | custom-call | tf_op jit(solution)/shard_map/split_matrix/pallas_call | solution.py:61
  65.2 0.0 copy-done.2
  65.2 0.6 dynamic_slice.7
  65.8 1.4 dynamic-slice_add_fusion
  67.2 14.0 %all-to-all-done.1 = f32[8,256,256]{2,1,0:T(8,128)S(1)} async-done(((f32[8,256,256]{2,1,0:T(8,128)}), f32[8,256,256]{2,1,0:T(8,128)S(1)}, u32[]{:S(2)}, u32[]{:S(2)}) %all-to-all-start.1) | async-done | bytes 2097184 | tf_op jit(solution)/shard_map/all_to_all | solution.py:172
  81.2 13.8 %solve_z.1 = f32[8,8,32,256]{3,2,1,0:T(8,128)S(1)} custom-call(f32[8,8,32,256]{3,2,1,0:T(8,128)S(1)} %bitcast.8, bf16[1024,1024]{1,0:T(8,128)(2,1)} %get-tuple-element.17.eh_ref, bf16[1024,1024]{1,0:T(8,128)(2,1)} %get-tuple-element.18.el_ref, bf16[1024,1024]{1,0:T(8,128)(2,1)} %get-tuple-element.19.oh_ref, bf16[1024,1024]{1,0:T(8,128)(2,1)} %get-tuple-element.20.ol_ref, ...), custom_call_target="tpu_custom_call" | custom-call | tf_op jit(solution)/shard_map/solve_z/pallas_call | solution.py:125
  95.0 29.8 %all_to_all.20.x_ref = f32[8,256,256]{2,1,0:T(8,128)S(1)} all-to-all(f32[8,256,256]{2,1,0:T(8,128)S(1)} %bitcast.10), channel_id=1, replica_groups=mesh['yh'=2,'core'=2,'z'=4,'yl'=2,'x'=4] {'x','core'}, dimensions={0} | all-to-all | bytes 4194304 | tf_op jit(solution)/shard_map/all_to_all | solution.py:174
  124.8 7.7 %backward_y.1 = f32[2,8,2,32,512]{4,3,2,1,0:T(8,128)S(1)} custom-call(f32[8,256,256]{2,1,0:T(8,128)S(1)} %all_to_all.20.x_ref, bf16[1024,1024]{1,0:T(8,128)(2,1)} %get-tuple-element.13.eh_ref, bf16[1024,1024]{1,0:T(8,128)(2,1)} %get-tuple-element.14.el_ref, bf16[1024,1024]{1,0:T(8,128)(2,1)} %get-tuple-element.15.oh_ref, ...), custom_call_target="tpu_custom_call" | custom-call | tf_op jit(solution)/shard_map/backward_y/pallas_call | solution.py:152
  132.5 33.6 %all_to_all.21 = f32[32,32,512]{2,1,0:T(8,128)S(1)} all-to-all(f32[32,32,512]{2,1,0:T(8,128)S(1)} %bitcast.11), channel_id=1, replica_groups=mesh['yh'=2,'core'=2,'z'=4,'yl'=2,'x'=4] {'yh','z','yl','core'}, dimensions={0} | all-to-all | bytes 4194304 | tf_op jit(solution)/shard_map/all_to_all | solution.py:176
  166.1 1.3 copy.12
Async XLA Ops:
  4.1 37.8 %all-to-all-start = ((f32[32,32,512]{2,1,0:T(8,128)}), f32[32,32,512]{2,1,0:T(8,128)S(1)}, u32[]{:S(2)}, u32[]{:S(2)}) async-start(f32[32,32,512]{2,1,0:T(8,128)} %bitcast.13), calls=%async_computation | async-start | bytes 4194304 | tf_op jit(solution)/shard_map/all_to_all | solution.py:166
  49.0 1.3 copy-start
  50.3 4.5 %copy-start.1 = (f32[2048]{0:T(1024)S(1)}, f32[2048]{0:T(1024)}, u32[]{:S(2)}) copy-start(f32[2048]{0:T(1024)} %param.17) | copy-start | bytes 24580
  50.3 30.9 %all-to-all-start.1 = ((f32[8,256,256]{2,1,0:T(8,128)}), f32[8,256,256]{2,1,0:T(8,128)S(1)}, u32[]{:S(2)}, u32[]{:S(2)}) async-start(f32[8,256,256]{2,1,0:T(8,128)} %copy-done), calls=%async_computation.1 | async-start | bytes 4194304 | tf_op jit(solution)/shard_map/all_to_all | solution.py:172
  60.5 4.7 %copy-start.2 = (f32[16]{0:T(128)S(1)}, f32[16]{0:T(128)}, u32[]{:S(2)}) copy-start(f32[16]{0:T(128)} %param.11) | copy-start | bytes 196

commit v2 on v1

v2 whole, which is shorter than its diff:
```python
import jax
import jax.numpy as jnp
from jax import lax
from jax.experimental import pallas as pl
from jax.experimental.pallas import tpu as pltpu
from jax.sharding import Mesh, PartitionSpec as P

F32 = jnp.float32
BF16 = jnp.bfloat16
TILE = 256
LANES = 128
HALF = 1024
ROWS = 256
SOURCE_LIMIT = 52
PREPARE_LIMIT = 8
KERNEL_LIMIT = 12
NARROW = ("yh", "core")
WIDE = ("z", "yl", "x")
VMEM = pl.BlockSpec(memory_space=pltpu.VMEM)
HBM = pl.BlockSpec(memory_space=pltpu.HBM)
NN = (((1,), (0,)), ((), ()))
NT = (((1,), (1,)), ((), ()))
TN = (((0,), (0,)), ((), ()))


def split(value):
    high = value.astype(BF16)
    low = (value - high.astype(F32)).astype(BF16)
    return high, low


def dot(left, right, dims):
    return lax.dot_general(left, right, dims, preferred_element_type=F32)


def product(left, right, dims):
    return (
        dot(left[0], right[0], dims)
        + dot(left[0], right[1], dims)
        + dot(left[1], right[0], dims)
    )


def mirror():
    row = lax.broadcasted_iota(jnp.int32, (TILE, TILE), 0)
    column = lax.broadcasted_iota(jnp.int32, (TILE, TILE), 1)
    return jnp.where(row + column == TILE - 1, 1.0, 0.0).astype(BF16)


def flip_lanes(value, flipper):
    high, low = split(value)
    return dot(high, flipper, NN) + dot(low, flipper, NN)


def flip_rows(value, flipper):
    high, low = split(value)
    return dot(flipper, high, NN) + dot(flipper, low, NN)


def low_quarter(across):
    core, yh = lax.axis_index("core"), lax.axis_index("yh")
    return jnp.bitwise_xor(jnp.bitwise_xor(core, yh), across)


def call(kernel, name, in_specs, out_specs, out_shape, scratch, limit, flops, **more):
    return pl.pallas_call(
        kernel,
        in_specs=in_specs,
        out_specs=out_specs,
        out_shape=out_shape,
        scratch_shapes=scratch,
        compiler_params=pltpu.CompilerParams(vmem_limit_bytes=limit << 20),
        cost_estimate=pl.CostEstimate(flops=flops, transcendentals=0, bytes_accessed=10 << 20),
        name=name,
        **more,
    )


def source_kernel(order, residual, counts, *refs):
    outs, residual_buffer, counts_buffer, sems = refs[:-3], *refs[-3:]
    me = lax.axis_index(NARROW)
    steps = [(i, part) for i in range(len(order)) for part in range(2)]

    def copies(step):
        i, part = step
        planes = pl.ds(4 * jnp.bitwise_xor(me, order[i]) + 2 * part, 2)
        slot = 2 * i + part
        yield pltpu.make_async_copy(residual.at[planes], residual_buffer.at[slot], sems.at[0, slot])
        yield pltpu.make_async_copy(counts.at[planes], counts_buffer.at[slot], sems.at[1, slot])

    for step in steps:
        for copy in copies(step):
            copy.start()
    for step in steps:
        for copy in copies(step):
            copy.wait()
        i, part = step
        slot = 2 * i + part
        value = residual_buffer[slot] + 0.3 * (counts_buffer[slot].astype(F32) - 2.0)
        outs[i][part * 128 : (part + 1) * 128] = value.reshape(128, 512)


def make_source(order, residual, counts):
    def kernel(*refs):
        source_kernel(order, *refs)

    count = len(order)
    return call(
        kernel,
        "make_source",
        [HBM] * 2,
        [VMEM] * count,
        [jax.ShapeDtypeStruct((ROWS, 512), F32)] * count,
        [
            pltpu.VMEM((2 * count, 2, 64, 512), F32),
            pltpu.VMEM((2 * count, 2, 64, 512), jnp.int32),
            pltpu.SemaphoreType.DMA((2, 2 * count)),
        ],
        SOURCE_LIMIT,
        1 << 20,
    )(residual, counts)


def prepare_kernel(*refs):
    matrices, outs, buffer, sems = refs[:4], refs[4:12], *refs[12:]
    steps = [(m, r) for m in range(4) for r in range(4)]

    def fetch(index):
        matrix, rows = steps[index]
        source = matrices[matrix].at[pl.ds(rows * TILE, TILE)]
        return pltpu.make_async_copy(source, buffer.at[index % 4], sems.at[index % 4])

    for index in range(3):
        fetch(index).start()
    for index, (matrix, rows) in enumerate(steps):
        if index + 3 < 16:
            fetch(index + 3).start()
        fetch(index).wait()
        high, low = split(buffer[index % 4])
        outs[2 * matrix][rows * TILE : (rows + 1) * TILE] = high
        outs[2 * matrix + 1][rows * TILE : (rows + 1) * TILE] = low


def prepare(*matrices):
    outs = call(
        prepare_kernel,
        "prepare",
        [HBM] * 4,
        [VMEM] * 8,
        [jax.ShapeDtypeStruct((HALF, HALF), BF16)] * 8,
        [pltpu.VMEM((4, TILE, HALF), F32), pltpu.SemaphoreType.DMA((4,))],
        PREPARE_LIMIT,
        4 << 30,
    )(*matrices)
    return outs[:4], outs[4:]


def send(block, d):
    return lax.ppermute(block, NARROW, [(n, n ^ d) for n in range(4)])


def forward_y_kernel(across, near_ref, far_ref, eh, el, oh, ol, *refs):
    held, out_ref, halves = refs[:-2], refs[-2], refs[-1]
    yh = lax.axis_index("yh")
    halves[yh] = near_ref[...]
    halves[1 - yh] = far_ref[...]
    flipper = mirror()
    sym, anti = [], []
    for part in range(2):
        low = halves[0, :, part * TILE : (part + 1) * TILE]
        high = flip_lanes(halves[1, :, (1 - part) * TILE : (2 - part) * TILE], flipper)
        sym.append(split(low + high))
        anti.append(split(low - high))
    rows = pl.ds(pl.multiple_of(512 * low_quarter(across), 512), 512)
    for base, sides, high, low in ((0, sym, eh, el), (4, anti, oh, ol)):
        left = tuple(jnp.concatenate([s[i] for s in sides], 1) for i in range(2))
        for block in range(4):
            lanes = slice(block * TILE, (block + 1) * TILE)
            result = product(left, (high[rows, lanes], low[rows, lanes]), NN)
            result = result.reshape(4, 64, TILE)
            if held:
                result = result + held[0][:, base + block]
            out_ref[:, base + block] = result


def forward_y(across, near, far, matrices, held):
    def kernel(*refs):
        forward_y_kernel(across, *refs)

    more = [] if held is None else [held]
    return call(
        kernel,
        "forward_y",
        [VMEM] * (6 + len(more)),
        VMEM,
        jax.ShapeDtypeStruct((4, 8, 64, TILE), F32),
        [pltpu.VMEM((2, ROWS, 512), F32)],
        KERNEL_LIMIT,
        2 << 30,
    )(near, far, *matrices, *more)


def pieces(value):
    high = value.astype(BF16)
    rest = value - high.astype(F32)
    middle = rest.astype(BF16)
    low = (rest - middle.astype(F32)).astype(BF16)
    return [high.astype(F32), middle.astype(F32), low.astype(F32)]


def solve_z_kernel(x_ref, eh, el, oh, ol, lamz_ref, lamy_ref, screen_ref, out_ref):
    flipper = mirror()
    place = lax.axis_index(WIDE)
    plane, modes = 4 * lax.axis_index(NARROW) + place // 8, place % 8
    shift = jnp.concatenate([lamy_ref[pl.ds(2 * modes + i, 1)] for i in range(2)], 1)
    shift = pieces(shift + screen_ref[plane])
    shift = jnp.concatenate(shift + [jnp.ones((1, TILE), F32)] * 3, 0).astype(BF16)
    sym, anti = [], []
    for block in range(4):
        low = x_ref[4 * block : 4 * block + 4].reshape(TILE, TILE)
        high = x_ref[28 - 4 * block : 32 - 4 * block].reshape(TILE, TILE)
        high = flip_rows(high, flipper)
        sym.append(split(low + high))
        anti.append(split(low - high))
    results = []
    for parity, sides, matrix in ((0, sym, (eh, el)), (1, anti, (oh, ol))):
        right = tuple(jnp.concatenate([s[i] for s in sides], 0) for i in range(2))
        pair = (matrix[0][...], matrix[1][...])
        spectral = product(pair, right, TN)
        lam = jnp.concatenate([lamz_ref[8 * parity + i : 8 * parity + i + 1] for i in range(8)], 1)
        lam = jnp.concatenate([jnp.ones((1, HALF), F32)] * 3 + pieces(lam), 0).astype(BF16)
        scaled = spectral / dot(lam, shift, TN)
        results.append(product(pair, split(scaled), NN))
    total = results[0] + results[1]
    rest = results[0] - results[1]
    for block in range(4):
        rows = slice(block * TILE, (block + 1) * TILE)
        out_ref[4 * block : 4 * block + 4] = total[rows].reshape(4, 64, TILE)
        flipped = flip_rows(rest[rows], flipper)
        out_ref[28 - 4 * block : 32 - 4 * block] = flipped.reshape(4, 64, TILE)


def solve_z(x, matrices, lam_z, lam_y, screening):
    return call(
        solve_z_kernel,
        "solve_z",
        [VMEM] * 7 + [pl.BlockSpec(memory_space=pltpu.SMEM)],
        VMEM,
        jax.ShapeDtypeStruct((32, 64, TILE), F32),
        [],
        KERNEL_LIMIT,
        6 << 30,
    )(x, *matrices, lam_z.reshape(16, LANES), lam_y.reshape(16, LANES), screening)


def backward_y_kernel(across, x_ref, eh, el, oh, ol, near_ref, far_ref, halves):
    flipper = mirror()
    sides = []
    for parity in range(2):
        blocks = [x_ref[:, 4 * parity + i].reshape(ROWS, TILE) for i in range(4)]
        sides.append(split(jnp.concatenate(blocks, 1)))
    start = 512 * low_quarter(across)
    for part in range(2):
        rows = pl.ds(pl.multiple_of(start + part * TILE, TILE), TILE)
        even = product(sides[0], (eh[rows], el[rows]), NT)
        odd = product(sides[1], (oh[rows], ol[rows]), NT)
        halves[0, :, part * TILE : (part + 1) * TILE] = even + odd
        flipped = flip_lanes(even - odd, flipper)
        halves[1, :, (1 - part) * TILE : (2 - part) * TILE] = flipped
    yh = lax.axis_index("yh")
    near_ref[...] = halves[yh]
    far_ref[...] = halves[1 - yh]


def backward_y(across, x, matrices):
    def kernel(*refs):
        backward_y_kernel(across, *refs)

    return call(
        kernel,
        "backward_y",
        [VMEM] * 5,
        [VMEM] * 2,
        [jax.ShapeDtypeStruct((ROWS, 512), F32)] * 2,
        [pltpu.VMEM((2, ROWS, 512), F32)],
        KERNEL_LIMIT,
        2 << 30,
    )(x, *matrices)


def place_kernel(order, *refs):
    blocks, out, sems = refs[: len(order)], refs[-2], refs[-1]
    me = lax.axis_index(NARROW)
    steps = [(i, part) for i in range(len(order)) for part in range(2)]

    def copy(i, part):
        start = ROWS * jnp.bitwise_xor(me, order[i]) + part * 128
        target = out.at[pl.ds(pl.multiple_of(start, 128), 128)]
        source = blocks[i].at[pl.ds(part * 128, 128)]
        return pltpu.make_async_copy(source, target, sems.at[i, part])

    for step in steps:
        copy(*step).start()
    for step in steps:
        copy(*step).wait()


def place(order, blocks, held):
    def kernel(*refs):
        place_kernel(order, *refs)

    more = [] if held is None else [held]
    return call(
        kernel,
        "place",
        [pl.BlockSpec(memory_space=pl.ANY)] * len(order) + [HBM] * len(more),
        HBM,
        jax.ShapeDtypeStruct((HALF, 512), F32),
        [pltpu.SemaphoreType.DMA((len(order), 2))],
        2,
        1 << 20,
        input_output_aliases={} if held is None else {len(order): 0},
    )(*blocks, *more)


def on_device(residual, counts, screening, even_y, odd_y, even_z, odd_z, lam_y, lam_z):
    (block2,) = make_source((2,), residual, counts)
    block3, block1, block0 = make_source((3, 1, 0), residual, counts)
    block2, block3, block1 = send(block2, 2), send(block3, 3), send(block1, 1)
    matrix_y, matrix_z = prepare(even_y, odd_y, even_z, odd_z)
    along = forward_y(1, block1, block2, matrix_y, None)
    along = forward_y(0, block0, block3, matrix_y, along)
    columns = lax.all_to_all(along.reshape(32, 64, TILE), WIDE, 0, 0, tiled=True)
    back = solve_z(columns, matrix_z, lam_z, lam_y, screening)
    rows = lax.all_to_all(back, WIDE, 0, 0, tiled=True).reshape(4, 8, 64, TILE)
    block1, block2 = backward_y(1, rows, matrix_y)
    block0, block3 = backward_y(0, rows, matrix_y)
    block2, block3, block1 = send(block2, 2), send(block3, 3), send(block1, 1)
    out = place((0, 1, 2), (block0, block1, block2), None)
    out = place((3,), (block3,), out)
    return out.reshape(16, 64, 512)


def solution(mesh):
    fine = Mesh(mesh.devices.reshape(2, 2, 4, 2, 4), ("yh", "core", "z", "yl", "x"))
    split_spec = P(None, WIDE, NARROW)
    return jax.shard_map(
        on_device,
        mesh=fine,
        in_specs=(split_spec, split_spec) + (P(),) * 7,
        out_specs=split_spec,
        check_vma=False,
    )
```

time: 168 us -> 143 us (0.85)
  Pallas kernels: 47.7 us -> 29.2 us
  other arithmetic: 5.44 us -> 0 us
  blocking collectives: 63.3 us -> 68.7 us
  starting transfers between devices: 14.1 us -> 10.6 us
  waiting for transfers between devices: 32.6 us -> 29.7 us
    all_to_all x2 -> x0, waiting for transfers between devices: 32.6 us -> none  [the longest x1 18.6 us: on_device(): lax.all_to_all(source.reshape(32, 32, 512), GATHER_Y, 0, 0, tiled=True)]
    ppermute x0 -> x6, waiting for transfers between devices: none -> 29.7 us  [send(): return lax.ppermute(block, NARROW, [(n, n ^ d) for n in range(4)])]
    pallas_call x7 -> x10, Pallas kernels: 47.7 us -> 29.2 us  [the longest x1 11.4 us: solve_z(): call(solve_z_kernel, 'solve_z', [VMEM] * 7 + [pl.BlockSpec(memory_space=p...]
    all_to_all x2 -> x0, starting transfers between devices: 14.1 us -> none  [the longest x1 9.6 us: on_device(): lax.all_to_all(source.reshape(32, 32, 512), GATHER_Y, 0, 0, tiled=True)]
    ppermute x0 -> x6, starting transfers between devices: none -> 10.6 us  [send(): return lax.ppermute(block, NARROW, [(n, n ^ d) for n in range(4)])]
    add x2 -> x0, other arithmetic: 5.44 us -> none  [the longest x1 4.05 us: on_device(): source = residual + 0.3 * (counts.astype(F32) - 2.0)]
    all_to_all x2, blocking collectives: 63.3 us -> 68.7 us  [the longest x1 36.7 us: on_device(): lax.all_to_all(along.reshape(32, 64, TILE), WIDE, 0, 0, tiled=True)]
    unnamed x7 -> x14, local copies, waits for them, and re-layouts: 2.64 us -> 4.4 us
  transfers between devices with their start and end apart: 2 -> 6, of which waited for: 2 -> 4; matrix products, arithmetic and copies ran while one was open for 2% -> 0% of each run, Pallas kernels for 11% -> 8%
where the time goes in v2:
time: 143 us
  blocking collectives  68.7 us (48%)
  waiting for transfers between devices  29.7 us (21%)
  Pallas kernels  29.2 us (20%)
  starting transfers between devices  10.6 us (7%)
  local copies, waits for them, and re-layouts  4.4 us (3%)
    all_to_all x1, blocking collectives, on_device(): lax.all_to_all(along.reshape(32, 64, TILE), WIDE, 0, 0, tiled=True)  36.7 us
    all_to_all x1, blocking collectives, on_device(): rows = lax.all_to_all(back, WIDE, 0, 0, tiled=True).reshape(4, 8, 64, TILE)  32 us
    ppermute x6, waiting for transfers between devices, send(): return lax.ppermute(block, NARROW, [(n, n ^ d) for n in range(4)])  29.7 us
    pallas_call x1, Pallas kernels, solve_z(): call(solve_z_kernel, 'solve_z', [VMEM] * 7 + [pl.BlockSpec(memory_space=p...  11.4 us
    ppermute x6, starting transfers between devices, send(): return lax.ppermute(block, NARROW, [(n, n ^ d) for n in range(4)])  10.6 us
    pallas_call x2, Pallas kernels, backward_y(): call(kernel, 'backward_y', [VMEM] * 5, [VMEM] * 2, [jax.ShapeDtypeStruct(...  4.78 us
    unnamed x14, local copies, waits for them, and re-layouts  4.4 us
    pallas_call x2, Pallas kernels, forward_y(): call(kernel, 'forward_y', [VMEM] * (6 + len(more)), VMEM, jax.ShapeDtypeS...  4.25 us
  transfers between devices with their start and end apart: 6, of which 4 were waited for; matrix products, arithmetic and copies ran while one was open for 0% of the time, Pallas kernels for 8%

profile of v2, /device:TPU:1, one launch (start us, length us, event | category | flops | bytes accessed | tf_op | source)
XLA Modules:
  0.0 143.0 jit_solution(10903777784208633876)
XLA Ops:
  0.0 1.4 make_source.3
  1.4 3.8 %collective-permute-start.2 = (f32[256,512]{1,0:T(8,128)S(1)}, f32[256,512]{1,0:T(8,128)S(1)}, u32[]{:S(2)}, u32[]{:S(2)}) collective-permute-start(f32[256,512]{1,0:T(8,128)S(1)} %make_source.3), channel_id=1, source_target_pairs={{0,64},{32,96},{64,0},{96,32},{1,65},{33,97},{65,1},{97,33},{2,66}... | collective-permute-start | bytes 1572872 | tf_op jit(solution)/shard_map/ppermute | solution.py:159
  5.3 2.0 %make_source.2 = (f32[256,512]{1,0:T(8,128)S(1)}, f32[256,512]{1,0:T(8,128)S(1)}, f32[256,512]{1,0:T(8,128)S(1)}) custom-call(f32[16,64,512]{2,1,0:T(8,128)} %refs_0_.5, s32[16,64,512]{2,1,0:T(8,128)} %refs_1_.5), custom_call_target="tpu_custom_call" | custom-call | flops 1048576 | bytes 10485760 | tf_op jit(solution)/shard_map/make_source/pallas_call | solution.py:108
  7.2 1.0 collective-permute-start.1
  8.3 0.2 collective-permute-start
  8.5 2.2 %copy-done.2 = f32[1024,1024]{1,0:T(8,128)S(1)} copy-done((f32[1024,1024]{1,0:T(8,128)S(1)}, f32[1024,1024]{1,0:T(8,128)}, u32[]{:S(2)}) %copy-start.2) | copy-done | bytes 4194328
  10.7 2.2 %copy-done.3 = f32[1024,1024]{1,0:T(8,128)S(1)} copy-done((f32[1024,1024]{1,0:T(8,128)S(1)}, f32[1024,1024]{1,0:T(8,128)}, u32[]{:S(2)}) %copy-start.3) | copy-done | bytes 4194328
  12.9 3.4 %prepare.1 = (bf16[1024,1024]{1,0:T(8,128)(2,1)S(1)}, bf16[1024,1024]{1,0:T(8,128)(2,1)S(1)}, bf16[1024,1024]{1,0:T(8,128)(2,1)S(1)}, bf16[1024,1024]{1,0:T(8,12...) custom-call(f32[1024,1024]{1,0:T(8,128)S(1)} %copy-done, ...), custom_call_target="tpu_custom_call" | custom-call | flops 4294967296 | bytes 10485760 | tf_op jit(solution)/shard_map/prepare/pallas_call | solution.py:145
  16.3 0.3 collective-permute-done.2.refs_1_
  16.6 2.1 %forward_y.2.refs_6_ = f32[4,8,64,256]{3,2,1,0:T(8,128)S(1)} custom-call(f32[256,512]{1,0:T(8,128)S(1)} %collective-permute-done.1.refs_0_, f32[256,512]{1,0:T(8,128)S(1)} %collective-permute-done.2.refs_1_, bf16[1024,1024]{1,0:T(8,128)(2,1)S(1)} %get-tuple-element.22.refs_2_.refs_1_, bf16[1024,1024]{1,0:T(8,128)(2,1)S(1)} %get-tuple-element.23.refs_3_.refs_2_, ...), custom_call_target="tpu_custom_call" | custom-call | flops 2147483648 | bytes 10485760 | tf_op jit(solution)/shard_map/forward_y/pallas_call | solution.py:191
  18.8 9.9 %collective-permute-done.refs_1_ = f32[256,512]{1,0:T(8,128)S(1)} collective-permute-done((f32[256,512]{1,0:T(8,128)S(1)}, f32[256,512]{1,0:T(8,128)S(1)}, u32[]{:S(2)}, u32[]{:S(2)}) %collective-permute-start) | collective-permute-done | bytes 524320 | tf_op jit(solution)/shard_map/ppermute | solution.py:159
  28.7 2.1 %forward_y.3 = f32[4,8,64,256]{3,2,1,0:T(8,128)S(1)} custom-call(f32[256,512]{1,0:T(8,128)S(1)} %get-tuple-element.20.refs_0_, f32[256,512]{1,0:T(8,128)S(1)} %collective-permute-done.refs_1_, bf16[1024,1024]{1,0:T(8,128)(2,1)S(1)} %get-tuple-element.22.refs_2_.refs_1_, bf16[1024,1024]{1,0:T(8,128)(2,1)S(1)} %get-tuple-element.23.refs_3_.refs_2_, ...), custom_call_target="tpu_custom_call" | custom-call | flops 2147483648 | bytes 10485760 | tf_op jit(solution)/shard_map/forward_y/pallas_call | solution.py:191
  30.8 36.7 %all_to_all.10.x_ref = f32[32,64,256]{2,1,0:T(8,128)S(1)} all-to-all(f32[32,64,256]{2,1,0:T(8,128)S(1)} %bitcast.7), channel_id=1, replica_groups=mesh['yh'=2,'core'=2,'z'=4,'yl'=2,'x'=4] {'z','yl','x'}, dimensions={0} | all-to-all | bytes 4194304 | tf_op jit(solution)/shard_map/all_to_all | solution.py:333
  67.6 11.4 %solve_z.1 = f32[32,64,256]{2,1,0:T(8,128)S(1)} custom-call(f32[32,64,256]{2,1,0:T(8,128)S(1)} %all_to_all.10.x_ref, bf16[1024,1024]{1,0:T(8,128)(2,1)S(1)} %get-tuple-element.27.eh, bf16[1024,1024]{1,0:T(8,128)(2,1)S(1)} %get-tuple-element.28.el, bf16[1024,1024]{1,0:T(8,128)(2,1)S(1)} %get-tuple-element.29.oh, bf16[1024,1024]{1,0:T(8,128)(2,1)S(1)} %get-tuple-element.30.ol, ...), custom_call_target="tpu_custom_call" | custom-call | flops 6442450944 | bytes 10485760 | tf_op jit(solution)/shard_map/solve_z/pallas_call | solution.py:244
  79.0 32.0 %all_to_all.11 = f32[32,64,256]{2,1,0:T(8,128)S(1)} all-to-all(f32[32,64,256]{2,1,0:T(8,128)S(1)} %solve_z.1), channel_id=1, replica_groups=mesh['yh'=2,'core'=2,'z'=4,'yl'=2,'x'=4] {'z','yl','x'}, dimensions={0} | all-to-all | bytes 4194304 | tf_op jit(solution)/shard_map/all_to_all | solution.py:335
  111.0 2.4 %backward_y.3 = (f32[256,512]{1,0:T(8,128)S(1)}, f32[256,512]{1,0:T(8,128)S(1)}) custom-call(f32[4,8,64,256]{3,2,1,0:T(8,128)S(1)} %bitcast.5, bf16[1024,1024]{1,0:T(8,128)(2,1)S(1)} %get-tuple-element.22.refs_2_.refs_1_, bf16[1024,1024]{1,0:T(8,128)(2,1)S(1)} %get-tuple-element.23.refs_3_.refs_2_, bf16[1024,1024]{1,0:T(8,128)(2,1)S(1)} %get-tuple-element.24.refs_4_.refs_3_, ...), custom_call_target="tpu_custom_call" | custom-call | flops 2147483648 | bytes 10485760 | tf_op jit(solution)/shard_map/backward_y/pallas_call | solution.py:279
  113.4 2.2 %collective-permute-start.4 = (f32[256,512]{1,0:T(8,128)S(1)}, f32[256,512]{1,0:T(8,128)S(1)}, u32[]{:S(2)}, u32[]{:S(2)}) collective-permute-start(f32[256,512]{1,0:T(8,128)S(1)} %get-tuple-element.33), channel_id=1, source_target_pairs={{0,32},{32,0},{64,96},{96,64},{1,33},{33,1},{65,97},{97,65},{2,34}... | collective-permute-start | bytes 1572872 | tf_op jit(solution)/shard_map/ppermute | solution.py:159
  115.6 2.6 %collective-permute-start.5 = (f32[256,512]{1,0:T(8,128)S(1)}, f32[256,512]{1,0:T(8,128)S(1)}, u32[]{:S(2)}, u32[]{:S(2)}) collective-permute-start(f32[256,512]{1,0:T(8,128)S(1)} %get-tuple-element.34), channel_id=1, source_target_pairs={{0,64},{32,96},{64,0},{96,32},{1,65},{33,97},{65,1},{97,33},{2,66}... | collective-permute-start | bytes 1572872 | tf_op jit(solution)/shard_map/ppermute | solution.py:159
  118.2 2.4 %backward_y.2 = (f32[256,512]{1,0:T(8,128)S(1)}, f32[256,512]{1,0:T(8,128)S(1)}) custom-call(f32[4,8,64,256]{3,2,1,0:T(8,128)S(1)} %bitcast.6, bf16[1024,1024]{1,0:T(8,128)(2,1)S(1)} %get-tuple-element.22.refs_2_.refs_1_, bf16[1024,1024]{1,0:T(8,128)(2,1)S(1)} %get-tuple-element.23.refs_3_.refs_2_, bf16[1024,1024]{1,0:T(8,128)(2,1)S(1)} %get-tuple-element.24.refs_4_.refs_3_, ...), custom_call_target="tpu_custom_call" | custom-call | flops 2147483648 | bytes 10485760 | tf_op jit(solution)/shard_map/backward_y/pallas_call | solution.py:279
  120.6 0.7 collective-permute-start.3
  121.3 9.3 %collective-permute-done.5.refs_2_ = f32[256,512]{1,0:T(8,128)S(1)} collective-permute-done((f32[256,512]{1,0:T(8,128)S(1)}, f32[256,512]{1,0:T(8,128)S(1)}, u32[]{:S(2)}, u32[]{:S(2)}) %collective-permute-start.5) | collective-permute-done | bytes 524320 | tf_op jit(solution)/shard_map/ppermute | solution.py:159
  130.6 1.2 place.2.refs_1_
  131.8 10.2 %collective-permute-done.3.refs_0_ = f32[256,512]{1,0:T(8,128)S(1)} collective-permute-done((f32[256,512]{1,0:T(8,128)S(1)}, f32[256,512]{1,0:T(8,128)S(1)}, u32[]{:S(2)}, u32[]{:S(2)}) %collective-permute-start.3) | collective-permute-done | bytes 524320 | tf_op jit(solution)/shard_map/ppermute | solution.py:159
  142.0 0.8 place.3
  (14 shorter events, 0.0 us)
Async XLA Ops:
  0.0 8.5 %copy-start.1 = (f32[1024,1024]{1,0:T(8,128)S(1)}, f32[1024,1024]{1,0:T(8,128)}, u32[]{:S(2)}) copy-start(f32[1024,1024]{1,0:T(8,128)} %refs_1_.4) | copy-start | bytes 12582916
  1.4 7.1 %copy-start = (f32[1024,1024]{1,0:T(8,128)S(1)}, f32[1024,1024]{1,0:T(8,128)}, u32[]{:S(2)}) copy-start(f32[1024,1024]{1,0:T(8,128)} %refs_0_.4) | copy-start | bytes 12582916
  1.4 15.2 %collective-permute-start.2 = (f32[256,512]{1,0:T(8,128)S(1)}, f32[256,512]{1,0:T(8,128)S(1)}, u32[]{:S(2)}, u32[]{:S(2)}) collective-permute-start(f32[256,512]{1,0:T(8,128)S(1)} %make_source.3), channel_id=1, source_target_pairs={{0,64},{32,96},{64,0},{96,32},{1,65},{33,97},{65,1},{97,33},{2,66}... | collective-permute-start | bytes 1572872 | tf_op jit(solution)/shard_map/ppermute | solution.py:159
  7.2 9.4 %collective-permute-start.1 = (f32[256,512]{1,0:T(8,128)S(1)}, f32[256,512]{1,0:T(8,128)S(1)}, u32[]{:S(2)}, u32[]{:S(2)}) collective-permute-start(f32[256,512]{1,0:T(8,128)S(1)} %get-tuple-element.26), channel_id=1, source_target_pairs={{0,32},{32,0},{64,96},{96,64},{1,33},{33,1},{65,97},{97,65},{2,34}... | collective-permute-start | bytes 1572872 | tf_op jit(solution)/shard_map/ppermute | solution.py:159
  8.3 20.4 %collective-permute-start = (f32[256,512]{1,0:T(8,128)S(1)}, f32[256,512]{1,0:T(8,128)S(1)}, u32[]{:S(2)}, u32[]{:S(2)}) collective-permute-start(f32[256,512]{1,0:T(8,128)S(1)} %get-tuple-element.21), channel_id=1, source_target_pairs={{0,96},{32,64},{64,32},{96,0},{1,97},{33,65},{65,33},{97,1},{2,98}... | collective-permute-start | bytes 1572872 | tf_op jit(solution)/shard_map/ppermute | solution.py:159
  8.5 2.2 %copy-start.2 = (f32[1024,1024]{1,0:T(8,128)S(1)}, f32[1024,1024]{1,0:T(8,128)}, u32[]{:S(2)}) copy-start(f32[1024,1024]{1,0:T(8,128)} %refs_2_.1) | copy-start | bytes 12582916
  10.7 2.2 %copy-start.3 = (f32[1024,1024]{1,0:T(8,128)S(1)}, f32[1024,1024]{1,0:T(8,128)}, u32[]{:S(2)}) copy-start(f32[1024,1024]{1,0:T(8,128)} %refs_3_.1) | copy-start | bytes 12582916
  30.8 36.8 %copy-start.4 = (f32[2048]{0:T(1024)S(1)}, f32[2048]{0:T(1024)}, u32[]{:S(2)}) copy-start(f32[2048]{0:T(1024)} %param.17) | copy-start | bytes 24580
  30.8 36.8 %copy-start.5 = (f32[2048]{0:T(1024)S(1)}, f32[2048]{0:T(1024)}, u32[]{:S(2)}) copy-start(f32[2048]{0:T(1024)} %param.16) | copy-start | bytes 24580
  30.8 36.8 %copy-start.6 = (f32[16]{0:T(128)S(1)}, f32[16]{0:T(128)}, u32[]{:S(2)}) copy-start(f32[16]{0:T(128)} %screen_ref.1) | copy-start | bytes 196
  113.4 7.9 %collective-permute-start.4 = (f32[256,512]{1,0:T(8,128)S(1)}, f32[256,512]{1,0:T(8,128)S(1)}, u32[]{:S(2)}, u32[]{:S(2)}) collective-permute-start(f32[256,512]{1,0:T(8,128)S(1)} %get-tuple-element.33), channel_id=1, source_target_pairs={{0,32},{32,0},{64,96},{96,64},{1,33},{33,1},{65,97},{97,65},{2,34}... | collective-permute-start | bytes 1572872 | tf_op jit(solution)/shard_map/ppermute | solution.py:159
  115.6 15.0 %collective-permute-start.5 = (f32[256,512]{1,0:T(8,128)S(1)}, f32[256,512]{1,0:T(8,128)S(1)}, u32[]{:S(2)}, u32[]{:S(2)}) collective-permute-start(f32[256,512]{1,0:T(8,128)S(1)} %get-tuple-element.34), channel_id=1, source_target_pairs={{0,64},{32,96},{64,0},{96,32},{1,65},{33,97},{65,1},{97,33},{2,66}... | collective-permute-start | bytes 1572872 | tf_op jit(solution)/shard_map/ppermute | solution.py:159
  120.6 21.4 %collective-permute-start.3 = (f32[256,512]{1,0:T(8,128)S(1)}, f32[256,512]{1,0:T(8,128)S(1)}, u32[]{:S(2)}, u32[]{:S(2)}) collective-permute-start(f32[256,512]{1,0:T(8,128)S(1)} %get-tuple-element.31), channel_id=1, source_target_pairs={{0,96},{32,64},{64,32},{96,0},{1,97},{33,65},{65,33},{97,1},{2,98}... | collective-permute-start | bytes 1572872 | tf_op jit(solution)/shard_map/ppermute | solution.py:159

commit v3 on v2

--- a/solution.py
+++ b/solution.py
@@ -122,8 +122,8 @@
 
 
 def prepare_kernel(*refs):
-    matrices, outs, buffer, sems = refs[:4], refs[4:12], *refs[12:]
-    steps = [(m, r) for m in range(4) for r in range(4)]
+    matrices, outs, buffer, sems = refs[:2], refs[2:6], *refs[6:]
+    steps = [(m, r) for m in range(2) for r in range(4)]
 
     def fetch(index):
         matrix, rows = steps[index]
@@ -133,7 +133,7 @@
     for index in range(3):
         fetch(index).start()
     for index, (matrix, rows) in enumerate(steps):
-        if index + 3 < 16:
+        if index + 3 < 8:
             fetch(index + 3).start()
         fetch(index).wait()
         high, low = split(buffer[index % 4])
@@ -142,28 +142,32 @@
 
 
 def prepare(*matrices):
-    outs = call(
+    return call(
         prepare_kernel,
         "prepare",
-        [HBM] * 4,
-        [VMEM] * 8,
-        [jax.ShapeDtypeStruct((HALF, HALF), BF16)] * 8,
+        [HBM] * 2,
+        [VMEM] * 4,
+        [jax.ShapeDtypeStruct((HALF, HALF), BF16)] * 4,
         [pltpu.VMEM((4, TILE, HALF), F32), pltpu.SemaphoreType.DMA((4,))],
         PREPARE_LIMIT,
-        4 << 30,
+        2 << 30,
     )(*matrices)
-    return outs[:4], outs[4:]
-
-
-def send(block, d):
-    return lax.ppermute(block, NARROW, [(n, n ^ d) for n in range(4)])
-
-
-def forward_y_kernel(across, near_ref, far_ref, eh, el, oh, ol, *refs):
+
+
+def send(block, d, cores=(0, 1)):
+    return lax.ppermute(block, NARROW, [(n, n ^ d) for n in range(4) if n % 2 in cores])
+
+
+def forward_y_kernel(across, near_ref, far0_ref, far1_ref, eh, el, oh, ol, _, *refs):
     held, out_ref, halves = refs[:-2], refs[-2], refs[-1]
     yh = lax.axis_index("yh")
     halves[yh] = near_ref[...]
-    halves[1 - yh] = far_ref[...]
+    for core, far_ref in enumerate((far0_ref, far1_ref)):
+
+        @pl.when(lax.axis_index("core") == core)
+        def _(far_ref=far_ref):
+            halves[1 - yh] = far_ref[...]
+
     flipper = mirror()
     sym, anti = [], []
     for part in range(2):
@@ -183,7 +187,7 @@
             out_ref[:, base + block] = result
 
 
-def forward_y(across, near, far, matrices, held):
+def forward_y(across, near, far, matrices, token, held):
     def kernel(*refs):
         forward_y_kernel(across, *refs)
 
@@ -191,13 +195,13 @@
     return call(
         kernel,
         "forward_y",
-        [VMEM] * (6 + len(more)),
+        [VMEM] * (8 + len(more)),
         VMEM,
         jax.ShapeDtypeStruct((4, 8, 64, TILE), F32),
         [pltpu.VMEM((2, ROWS, 512), F32)],
         KERNEL_LIMIT,
         2 << 30,
-    )(near, far, *matrices, *more)
+    )(near, *far, *matrices, token, *more)
 
 
 def pieces(value):
@@ -324,18 +328,28 @@
 
 
 def on_device(residual, counts, screening, even_y, odd_y, even_z, odd_z, lam_y, lam_z):
-    (block2,) = make_source((2,), residual, counts)
-    block3, block1, block0 = make_source((3, 1, 0), residual, counts)
-    block2, block3, block1 = send(block2, 2), send(block3, 3), send(block1, 1)
-    matrix_y, matrix_z = prepare(even_y, odd_y, even_z, odd_z)
-    along = forward_y(1, block1, block2, matrix_y, None)
-    along = forward_y(0, block0, block3, matrix_y, along)
+    block3, block2 = make_source((3, 2), residual, counts)
+    block1, block0 = make_source((1, 0), residual, counts)
+    block3, block1, block0 = lax.optimization_barrier((send(block3, 1), block1, block0))
+    own0, sibling0 = send(block2, 2, (0,)), send(block3, 2, (0,))
+    block1 = send(block1, 1)
+    matrix_y, matrix_z = prepare(even_y, odd_y), prepare(even_z, odd_z)
+    block1, sibling0, own0, matrix_y, matrix_z = lax.optimization_barrier(
+        (block1, sibling0, own0, matrix_y, matrix_z)
+    )
+    token = send(sibling0[:8, :LANES], 1, (0,))
+    block2, block3, token = lax.optimization_barrier((block2, block3, token))
+    own1, sibling1 = send(block2, 2, (1,)), send(block3, 2, (1,))
+    along = forward_y(1, block1, (own0, own1), matrix_y, token, None)
+    along = forward_y(0, block0, (sibling0, sibling1), matrix_y, token, along)
     columns = lax.all_to_all(along.reshape(32, 64, TILE), WIDE, 0, 0, tiled=True)
     back = solve_z(columns, matrix_z, lam_z, lam_y, screening)
     rows = lax.all_to_all(back, WIDE, 0, 0, tiled=True).reshape(4, 8, 64, TILE)
     block1, block2 = backward_y(1, rows, matrix_y)
     block0, block3 = backward_y(0, rows, matrix_y)
-    block2, block3, block1 = send(block2, 2), send(block3, 3), send(block1, 1)
+    block2, block3 = send(block2, 2), send(block3, 2)
+    block1, block2 = lax.optimization_barrier((block1, block2))
+    block1, block3 = send(block1, 1), send(block3, 1)
     out = place((0, 1, 2), (block0, block1, block2), None)
     out = place((3,), (block3,), out)
     return out.reshape(16, 64, 512)

time: 143 us -> 134 us (0.937)
  blocking collectives: 68.7 us -> 52.3 us
  starting transfers between devices: 10.6 us -> 20.1 us
  local copies, waits for them, and re-layouts: 4.4 us -> 0.04 us
    all_to_all x1, blocking collectives: 32 us -> 21.5 us  [on_device(): rows = lax.all_to_all(back, WIDE, 0, 0, tiled=True).reshape(4, 8, 64, TILE)]
    ppermute x6 -> x11, starting transfers between devices: 10.6 us -> 20.1 us  [send(): lax.ppermute(block, NARROW, [(n, n ^ d) for n in range(4) if n % 2 in cor...]
    all_to_all x1, blocking collectives: 36.7 us -> 30.8 us  [on_device(): lax.all_to_all(along.reshape(32, 64, TILE), WIDE, 0, 0, tiled=True)]
    unnamed x14, local copies, waits for them, and re-layouts: 4.4 us -> 0.04 us
    ppermute x6 -> x11, waiting for transfers between devices: 29.7 us -> 30.7 us  [send(): lax.ppermute(block, NARROW, [(n, n ^ d) for n in range(4) if n % 2 in cor...]
    pallas_call x3 -> x4, Pallas kernels: 7.66 us -> 7.75 us  [the longest x2 4.29 us: forward_y(): call(kernel, 'forward_y', [VMEM] * (8 + len(more)), VMEM, jax.ShapeDtypeS...]
  transfers between devices with their start and end apart: 6 -> 11, of which waited for: 4 -> 6; matrix products, arithmetic and copies ran while one was open for 0% -> 0% of each run, Pallas kernels for 8% -> 8%
where the time goes in v3:
time: 134 us; the launch traced here: 133 us
  blocking collectives  52.3 us (39%)
  waiting for transfers between devices  30.7 us (23%)
  Pallas kernels  29.8 us (22%)
  starting transfers between devices  20.1 us (15%)
    all_to_all x1, blocking collectives, on_device(): lax.all_to_all(along.reshape(32, 64, TILE), WIDE, 0, 0, tiled=True)  30.8 us
    ppermute x11, waiting for transfers between devices, send(): lax.ppermute(block, NARROW, [(n, n ^ d) for n in range(4) if n % 2 in cor...  30.7 us
    all_to_all x1, blocking collectives, on_device(): rows = lax.all_to_all(back, WIDE, 0, 0, tiled=True).reshape(4, 8, 64, TILE)  21.5 us
    ppermute x11, starting transfers between devices, send(): lax.ppermute(block, NARROW, [(n, n ^ d) for n in range(4) if n % 2 in cor...  20.1 us
    pallas_call x1, Pallas kernels, solve_z(): call(solve_z_kernel, 'solve_z', [VMEM] * 7 + [pl.BlockSpec(memory_space=p...  11.4 us
    pallas_call x2, Pallas kernels, backward_y(): call(kernel, 'backward_y', [VMEM] * 5, [VMEM] * 2, [jax.ShapeDtypeStruct(...  4.86 us
    pallas_call x2, Pallas kernels, forward_y(): call(kernel, 'forward_y', [VMEM] * (8 + len(more)), VMEM, jax.ShapeDtypeS...  4.29 us
    pallas_call x2, Pallas kernels, make_source(): call(kernel, 'make_source', [HBM] * 2, [VMEM] * count, [jax.ShapeDtypeStr...  3.79 us
  transfers between devices with their start and end apart: 11, of which 6 were waited for; matrix products, arithmetic and copies ran while one was open for 0% of the time, Pallas kernels for 8%

profile of v3, /device:TPU:1, one launch (start us, length us, event | category | flops | bytes accessed | tf_op | source)
XLA Modules:
  0.0 133.3 jit_solution(17411160183128276291)
XLA Ops:
  0.0 1.8 %make_source.2 = (f32[256,512]{1,0:T(8,128)S(1)}, f32[256,512]{1,0:T(8,128)S(1)}) custom-call(f32[16,64,512]{2,1,0:T(8,128)} %refs_0_.5, s32[16,64,512]{2,1,0:T(8,128)} %refs_1_.5), custom_call_target="tpu_custom_call" | custom-call | flops 1048576 | bytes 10485760 | tf_op jit(solution)/shard_map/make_source/pallas_call | solution.py:108
  1.8 1.5 %collective-permute-start = (f32[256,512]{1,0:T(8,128)S(1)}, f32[256,512]{1,0:T(8,128)S(1)}, u32[]{:S(2)}, u32[]{:S(2)}) collective-permute-start(f32[256,512]{1,0:T(8,128)S(1)} %get-tuple-element.40), channel_id=1, source_target_pairs={{0,32},{32,0},{64,96},{96,64},{1,33},{33,1},{65,97},{97,65},{2,34}... | collective-permute-start | bytes 1572872 | tf_op jit(solution)/shard_map/ppermute | solution.py:158
  3.3 0.8 collective-permute-start.3
  4.1 2.0 %make_source.3 = (f32[256,512]{1,0:T(8,128)S(1)}, f32[256,512]{1,0:T(8,128)S(1)}) custom-call(f32[16,64,512]{2,1,0:T(8,128)} %refs_0_.5, s32[16,64,512]{2,1,0:T(8,128)} %refs_1_.5), custom_call_target="tpu_custom_call" | custom-call | flops 1048576 | bytes 10485760 | tf_op jit(solution)/shard_map/make_source/pallas_call | solution.py:108
  6.2 4.3 %collective-permute-start.1 = (f32[256,512]{1,0:T(8,128)S(1)}, f32[256,512]{1,0:T(8,128)S(1)}, u32[]{:S(2)}, u32[]{:S(2)}) collective-permute-start(f32[256,512]{1,0:T(8,128)S(1)} %get-tuple-element.44), channel_id=1, source_target_pairs={{0,32},{32,0},{64,96},{96,64},{1,33},{33,1},{65,97},{97,65},{2,34}... | collective-permute-start | bytes 1572872 | tf_op jit(solution)/shard_map/ppermute | solution.py:158
  11.2 1.7 %prepare.2 = (bf16[1024,1024]{1,0:T(8,128)(2,1)S(1)}, bf16[1024,1024]{1,0:T(8,128)(2,1)S(1)}, bf16[1024,1024]{1,0:T(8,128)(2,1)S(1)}, bf16[1024,1024]{1,0:T(8,128)(2,1)S(1)}) custom-call(f32[1024,1024]{1,0:T(8,128)S(1)} %copy-done, f32[1024,1024]{1,0:T(8,128)S(1)} %copy-done.1), custom_call_target="tpu_custom_call" | custom-call | flops 2147483648 | bytes 10485760 | tf_op jit(solution)/shard_map/prepare/pallas_call | solution.py:145
  13.0 1.7 %prepare.3 = (bf16[1024,1024]{1,0:T(8,128)(2,1)S(1)}, bf16[1024,1024]{1,0:T(8,128)(2,1)S(1)}, bf16[1024,1024]{1,0:T(8,128)(2,1)S(1)}, bf16[1024,1024]{1,0:T(8,128)(2,1)S(1)}) custom-call(f32[1024,1024]{1,0:T(8,128)S(1)} %copy-done.2, f32[1024,1024]{1,0:T(8,128)S(1)} %copy-done.3), custom_call_target="tpu_custom_call" | custom-call | flops 2147483648 | bytes 10485760 | tf_op jit(solution)/shard_map/prepare/pallas_call | solution.py:145
  14.7 1.3 collective-permute-start.4
  16.0 9.2 %collective-permute-done.4.refs_7_ = f32[8,128]{1,0:T(8,128)S(1)} collective-permute-done((f32[8,128]{1,0:T(8,128)S(1)}, f32[8,128]{1,0:T(8,128)S(1)}, u32[]{:S(2)}, u32[]{:S(2)}) %collective-permute-start.4) | collective-permute-done | bytes 4128 | tf_op jit(solution)/shard_map/ppermute | solution.py:158
  25.3 3.3 %collective-permute-start.6 = (f32[256,512]{1,0:T(8,128)S(1)}, f32[256,512]{1,0:T(8,128)S(1)}, u32[]{:S(2)}, u32[]{:S(2)}) collective-permute-start(f32[256,512]{1,0:T(8,128)S(1)} %get-tuple-element.64), channel_id=1, source_target_pairs={{32,96},{96,32},{33,97},{97,33},{34,98},{98,34},{35,99},{99,35},{3... | collective-permute-start | bytes 1572872 | tf_op jit(solution)/shard_map/ppermute | solution.py:158
  28.6 3.5 %collective-permute-start.5 = (f32[256,512]{1,0:T(8,128)S(1)}, f32[256,512]{1,0:T(8,128)S(1)}, u32[]{:S(2)}, u32[]{:S(2)}) collective-permute-start(f32[256,512]{1,0:T(8,128)S(1)} %collective-permute-done), channel_id=1, source_target_pairs={{32,96},{96,32},{33,97},{97,33},{34,98},{98,34},{35,99},{99,35},{3... | collective-permute-start | bytes 1572872 | tf_op jit(solution)/shard_map/ppermute | solution.py:158
  32.1 4.6 %collective-permute-done.6.refs_2_ = f32[256,512]{1,0:T(8,128)S(1)} collective-permute-done((f32[256,512]{1,0:T(8,128)S(1)}, f32[256,512]{1,0:T(8,128)S(1)}, u32[]{:S(2)}, u32[]{:S(2)}) %collective-permute-start.6) | collective-permute-done | bytes 524320 | tf_op jit(solution)/shard_map/ppermute | solution.py:158
  36.7 2.1 %forward_y.2.refs_8_ = f32[4,8,64,256]{3,2,1,0:T(8,128)S(1)} custom-call(f32[256,512]{1,0:T(8,128)S(1)} %collective-permute-done.1.refs_0_, f32[256,512]{1,0:T(8,128)S(1)} %collective-permute-done.3.refs_1_, f32[256,512]{1,0:T(8,128)S(1)} %collective-permute-done.6.refs_2_, bf16[1024,1024]{1,0:T(8,128)(2,1)S(1)} %get-tuple-element.57.refs_3_.refs_1_, ...), custom_call_target="tpu_custom_call" | custom-call | flops 2147483648 | bytes 10485760 | tf_op jit(solution)/shard_map/forward_y/pallas_call | solution.py:195
  38.8 3.5 %collective-permute-done.5.refs_2_ = f32[256,512]{1,0:T(8,128)S(1)} collective-permute-done((f32[256,512]{1,0:T(8,128)S(1)}, f32[256,512]{1,0:T(8,128)S(1)}, u32[]{:S(2)}, u32[]{:S(2)}) %collective-permute-start.5) | collective-permute-done | bytes 524320 | tf_op jit(solution)/shard_map/ppermute | solution.py:158
  42.3 2.2 %forward_y.3 = f32[4,8,64,256]{3,2,1,0:T(8,128)S(1)} custom-call(f32[256,512]{1,0:T(8,128)S(1)} %get-tuple-element.43.refs_0_, f32[256,512]{1,0:T(8,128)S(1)} %collective-permute-done.2.refs_1_, f32[256,512]{1,0:T(8,128)S(1)} %collective-permute-done.5.refs_2_, bf16[1024,1024]{1,0:T(8,128)(2,1)S(1)} %get-tuple-element.57.refs_3_.refs_1_, ...), custom_call_target="tpu_custom_call" | custom-call | flops 2147483648 | bytes 10485760 | tf_op jit(solution)/shard_map/forward_y/pallas_call | solution.py:195
  44.5 30.8 %all_to_all.10.x_ref = f32[32,64,256]{2,1,0:T(8,128)S(1)} all-to-all(f32[32,64,256]{2,1,0:T(8,128)S(1)} %bitcast.7), channel_id=1, replica_groups=mesh['yh'=2,'core'=2,'z'=4,'yl'=2,'x'=4] {'z','yl','x'}, dimensions={0} | all-to-all | bytes 4194304 | tf_op jit(solution)/shard_map/all_to_all | solution.py:345
  75.4 11.4 %solve_z.1 = f32[32,64,256]{2,1,0:T(8,128)S(1)} custom-call(f32[32,64,256]{2,1,0:T(8,128)S(1)} %all_to_all.10.x_ref, bf16[1024,1024]{1,0:T(8,128)(2,1)S(1)} %get-tuple-element.65.eh, bf16[1024,1024]{1,0:T(8,128)(2,1)S(1)} %get-tuple-element.66.el, bf16[1024,1024]{1,0:T(8,128)(2,1)S(1)} %get-tuple-element.67.oh, bf16[1024,1024]{1,0:T(8,128)(2,1)S(1)} %get-tuple-element.68.ol, ...), custom_call_target="tpu_custom_call" | custom-call | flops 6442450944 | bytes 10485760 | tf_op jit(solution)/shard_map/solve_z/pallas_call | solution.py:248
  86.8 21.5 %all_to_all.11 = f32[32,64,256]{2,1,0:T(8,128)S(1)} all-to-all(f32[32,64,256]{2,1,0:T(8,128)S(1)} %solve_z.1), channel_id=1, replica_groups=mesh['yh'=2,'core'=2,'z'=4,'yl'=2,'x'=4] {'z','yl','x'}, dimensions={0} | all-to-all | bytes 4194304 | tf_op jit(solution)/shard_map/all_to_all | solution.py:347
  108.2 2.4 %backward_y.3 = (f32[256,512]{1,0:T(8,128)S(1)}, f32[256,512]{1,0:T(8,128)S(1)}) custom-call(f32[4,8,64,256]{3,2,1,0:T(8,128)S(1)} %bitcast.5, bf16[1024,1024]{1,0:T(8,128)(2,1)S(1)} %get-tuple-element.57.refs_3_.refs_1_, bf16[1024,1024]{1,0:T(8,128)(2,1)S(1)} %get-tuple-element.58.refs_4_.refs_2_, bf16[1024,1024]{1,0:T(8,128)(2,1)S(1)} %get-tuple-element.59.refs_5_.refs_3_, ...), custom_call_target="tpu_custom_call" | custom-call | flops 2147483648 | bytes 10485760 | tf_op jit(solution)/shard_map/backward_y/pallas_call | solution.py:283
  110.7 4.6 %collective-permute-start.9 = (f32[256,512]{1,0:T(8,128)S(1)}, f32[256,512]{1,0:T(8,128)S(1)}, u32[]{:S(2)}, u32[]{:S(2)}) collective-permute-start(f32[256,512]{1,0:T(8,128)S(1)} %get-tuple-element.72), channel_id=1, source_target_pairs={{0,64},{32,96},{64,0},{96,32},{1,65},{33,97},{65,1},{97,33},{2,66}... | collective-permute-start | bytes 1572872 | tf_op jit(solution)/shard_map/ppermute | solution.py:158
  115.3 2.4 %backward_y.2 = (f32[256,512]{1,0:T(8,128)S(1)}, f32[256,512]{1,0:T(8,128)S(1)}) custom-call(f32[4,8,64,256]{3,2,1,0:T(8,128)S(1)} %bitcast.6, bf16[1024,1024]{1,0:T(8,128)(2,1)S(1)} %get-tuple-element.57.refs_3_.refs_1_, bf16[1024,1024]{1,0:T(8,128)(2,1)S(1)} %get-tuple-element.58.refs_4_.refs_2_, bf16[1024,1024]{1,0:T(8,128)(2,1)S(1)} %get-tuple-element.59.refs_5_.refs_3_, ...), custom_call_target="tpu_custom_call" | custom-call | flops 2147483648 | bytes 10485760 | tf_op jit(solution)/shard_map/backward_y/pallas_call | solution.py:283
  117.8 7.0 %collective-permute-done.9.refs_2_ = f32[256,512]{1,0:T(8,128)S(1)} collective-permute-done((f32[256,512]{1,0:T(8,128)S(1)}, f32[256,512]{1,0:T(8,128)S(1)}, u32[]{:S(2)}, u32[]{:S(2)}) %collective-permute-start.9) | collective-permute-done | bytes 524320 | tf_op jit(solution)/shard_map/ppermute | solution.py:158
  124.8 5.6 %collective-permute-done.7 = f32[256,512]{1,0:T(8,128)S(1)} collective-permute-done((f32[256,512]{1,0:T(8,128)S(1)}, f32[256,512]{1,0:T(8,128)S(1)}, u32[]{:S(2)}, u32[]{:S(2)}) %collective-permute-start.7) | collective-permute-done | bytes 524320 | tf_op jit(solution)/shard_map/ppermute | solution.py:158
  130.4 1.2 place.2.refs_1_
  (26 shorter events, 2.4 us)
Async XLA Ops:
  0.0 11.2 %copy-start.1 = (f32[1024,1024]{1,0:T(8,128)S(1)}, f32[1024,1024]{1,0:T(8,128)}, u32[]{:S(2)}) copy-start(f32[1024,1024]{1,0:T(8,128)} %refs_1_.6) | copy-start | bytes 12582916
  1.8 4.4 %collective-permute-start = (f32[256,512]{1,0:T(8,128)S(1)}, f32[256,512]{1,0:T(8,128)S(1)}, u32[]{:S(2)}, u32[]{:S(2)}) collective-permute-start(f32[256,512]{1,0:T(8,128)S(1)} %get-tuple-element.40), channel_id=1, source_target_pairs={{0,32},{32,0},{64,96},{96,64},{1,33},{33,1},{65,97},{97,65},{2,34}... | collective-permute-start | bytes 1572872 | tf_op jit(solution)/shard_map/ppermute | solution.py:158
  3.3 7.9 %copy-start = (f32[1024,1024]{1,0:T(8,128)S(1)}, f32[1024,1024]{1,0:T(8,128)}, u32[]{:S(2)}) copy-start(f32[1024,1024]{1,0:T(8,128)} %refs_0_.6) | copy-start | bytes 12582916
  3.3 11.4 %collective-permute-start.3 = (f32[256,512]{1,0:T(8,128)S(1)}, f32[256,512]{1,0:T(8,128)S(1)}, u32[]{:S(2)}, u32[]{:S(2)}) collective-permute-start(f32[256,512]{1,0:T(8,128)S(1)} %get-tuple-element.64), channel_id=1, source_target_pairs={{0,64},{64,0},{1,65},{65,1},{2,66},{66,2},{3,67},{67,3},{4,68},{68... | collective-permute-start | bytes 1572872 | tf_op jit(solution)/shard_map/ppermute | solution.py:158
  6.1 6.8 %copy-start.2 = (f32[1024,1024]{1,0:T(8,128)S(1)}, f32[1024,1024]{1,0:T(8,128)}, u32[]{:S(2)}) copy-start(f32[1024,1024]{1,0:T(8,128)} %refs_0_.7) | copy-start | bytes 12582916
  6.2 6.8 %copy-start.3 = (f32[1024,1024]{1,0:T(8,128)S(1)}, f32[1024,1024]{1,0:T(8,128)}, u32[]{:S(2)}) copy-start(f32[1024,1024]{1,0:T(8,128)} %refs_1_.7) | copy-start | bytes 12582916
  6.2 8.5 %collective-permute-start.1 = (f32[256,512]{1,0:T(8,128)S(1)}, f32[256,512]{1,0:T(8,128)S(1)}, u32[]{:S(2)}, u32[]{:S(2)}) collective-permute-start(f32[256,512]{1,0:T(8,128)S(1)} %get-tuple-element.44), channel_id=1, source_target_pairs={{0,32},{32,0},{64,96},{96,64},{1,33},{33,1},{65,97},{97,65},{2,34}... | collective-permute-start | bytes 1572872 | tf_op jit(solution)/shard_map/ppermute | solution.py:158
  10.5 4.2 %collective-permute-start.2 = (f32[256,512]{1,0:T(8,128)S(1)}, f32[256,512]{1,0:T(8,128)S(1)}, u32[]{:S(2)}, u32[]{:S(2)}) collective-permute-start(f32[256,512]{1,0:T(8,128)S(1)} %collective-permute-done), channel_id=1, source_target_pairs={{0,64},{64,0},{1,65},{65,1},{2,66},{66,2},{3,67},{67,3},{4,68},{68... | collective-permute-start | bytes 1572872 | tf_op jit(solution)/shard_map/ppermute | solution.py:158
  14.7 10.5 %collective-permute-start.4 = (f32[8,128]{1,0:T(8,128)S(1)}, f32[8,128]{1,0:T(8,128)S(1)}, u32[]{:S(2)}, u32[]{:S(2)}) collective-permute-start(f32[8,128]{1,0:T(8,128)S(1)} %slice.3), channel_id=1, source_target_pairs={{0,32},{64,96},{1,33},{65,97},{2,34},{66,98},{3,35},{67,99},{4,36}... | collective-permute-start | bytes 12296 | tf_op jit(solution)/shard_map/ppermute | solution.py:158
  25.3 11.4 %collective-permute-start.6 = (f32[256,512]{1,0:T(8,128)S(1)}, f32[256,512]{1,0:T(8,128)S(1)}, u32[]{:S(2)}, u32[]{:S(2)}) collective-permute-start(f32[256,512]{1,0:T(8,128)S(1)} %get-tuple-element.64), channel_id=1, source_target_pairs={{32,96},{96,32},{33,97},{97,33},{34,98},{98,34},{35,99},{99,35},{3... | collective-permute-start | bytes 1572872 | tf_op jit(solution)/shard_map/ppermute | solution.py:158
  28.6 13.7 %collective-permute-start.5 = (f32[256,512]{1,0:T(8,128)S(1)}, f32[256,512]{1,0:T(8,128)S(1)}, u32[]{:S(2)}, u32[]{:S(2)}) collective-permute-start(f32[256,512]{1,0:T(8,128)S(1)} %collective-permute-done), channel_id=1, source_target_pairs={{32,96},{96,32},{33,97},{97,33},{34,98},{98,34},{35,99},{99,35},{3... | collective-permute-start | bytes 1572872 | tf_op jit(solution)/shard_map/ppermute | solution.py:158
  44.5 30.9 %copy-start.4 = (f32[2048]{0:T(1024)S(1)}, f32[2048]{0:T(1024)}, u32[]{:S(2)}) copy-start(f32[2048]{0:T(1024)} %param.17) | copy-start | bytes 24580
  44.5 30.9 %copy-start.5 = (f32[2048]{0:T(1024)S(1)}, f32[2048]{0:T(1024)}, u32[]{:S(2)}) copy-start(f32[2048]{0:T(1024)} %param.16) | copy-start | bytes 24580
  44.5 30.9 %copy-start.6 = (f32[16]{0:T(128)S(1)}, f32[16]{0:T(128)}, u32[]{:S(2)}) copy-start(f32[16]{0:T(128)} %screen_ref.1) | copy-start | bytes 196
  110.7 14.2 %collective-permute-start.9 = (f32[256,512]{1,0:T(8,128)S(1)}, f32[256,512]{1,0:T(8,128)S(1)}, u32[]{:S(2)}, u32[]{:S(2)}) collective-permute-start(f32[256,512]{1,0:T(8,128)S(1)} %get-tuple-element.72), channel_id=1, source_target_pairs={{0,64},{32,96},{64,0},{96,32},{1,65},{33,97},{65,1},{97,33},{2,66}... | collective-permute-start | bytes 1572872 | tf_op jit(solution)/shard_map/ppermute | solution.py:158
  117.7 12.7 %collective-permute-start.7 = (f32[256,512]{1,0:T(8,128)S(1)}, f32[256,512]{1,0:T(8,128)S(1)}, u32[]{:S(2)}, u32[]{:S(2)}) collective-permute-start(f32[256,512]{1,0:T(8,128)S(1)} %get-tuple-element.69), channel_id=1, source_target_pairs={{0,64},{32,96},{64,0},{96,32},{1,65},{33,97},{65,1},{97,33},{2,66}... | collective-permute-start | bytes 1572872 | tf_op jit(solution)/shard_map/ppermute | solution.py:158
  124.8 5.6 %collective-permute-start.10 = (f32[256,512]{1,0:T(8,128)S(1)}, f32[256,512]{1,0:T(8,128)S(1)}, u32[]{:S(2)}, u32[]{:S(2)}) collective-permute-start(f32[256,512]{1,0:T(8,128)S(1)} %get-tuple-element.73), channel_id=1, source_target_pairs={{0,32},{32,0},{64,96},{96,64},{1,33},{33,1},{65,97},{97,65},{2,34}... | collective-permute-start | bytes 1572872 | tf_op jit(solution)/shard_map/ppermute | solution.py:158
  130.4 1.9 %collective-permute-start.8 = (f32[256,512]{1,0:T(8,128)S(1)}, f32[256,512]{1,0:T(8,128)S(1)}, u32[]{:S(2)}, u32[]{:S(2)}) collective-permute-start(f32[256,512]{1,0:T(8,128)S(1)} %collective-permute-done.7), channel_id=1, source_target_pairs={{0,32},{32,0},{64,96},{96,64},{1,33},{33,1},{65,97},{97,65},{2,34}... | collective-permute-start | bytes 1572872 | tf_op jit(solution)/shard_map/ppermute | solution.py:158

commit v4 on v3

v4 whole, which is shorter than its diff:
```python
import jax
import jax.numpy as jnp
from jax import lax
from jax.experimental import pallas as pl
from jax.experimental.pallas import tpu as pltpu
from jax.sharding import Mesh, PartitionSpec as P

F32 = jnp.float32
BF16 = jnp.bfloat16
TILE = 256
LANES = 128
HALF = 1024
ROWS = 256
SOURCE_LIMIT = 52
PREPARE_LIMIT = 8
KERNEL_LIMIT = 12
NARROW = ("yh", "core")
WIDE = ("z", "x")
PLACES = ("yh", "core", "yl")
VMEM = pl.BlockSpec(memory_space=pltpu.VMEM)
HBM = pl.BlockSpec(memory_space=pltpu.HBM)
NN = (((1,), (0,)), ((), ()))
NT = (((1,), (1,)), ((), ()))
TN = (((0,), (0,)), ((), ()))


def split(value):
    high = value.astype(BF16)
    low = (value - high.astype(F32)).astype(BF16)
    return high, low


def dot(left, right, dims):
    return lax.dot_general(left, right, dims, preferred_element_type=F32)


def product(left, right, dims):
    return (
        dot(left[0], right[0], dims)
        + dot(left[0], right[1], dims)
        + dot(left[1], right[0], dims)
    )


def mirror():
    row = lax.broadcasted_iota(jnp.int32, (TILE, TILE), 0)
    column = lax.broadcasted_iota(jnp.int32, (TILE, TILE), 1)
    return jnp.where(row + column == TILE - 1, 1.0, 0.0).astype(BF16)


def flip_lanes(value, flipper):
    high, low = split(value)
    return dot(high, flipper, NN) + dot(low, flipper, NN)


def flip_rows(value, flipper):
    high, low = split(value)
    return dot(flipper, high, NN) + dot(flipper, low, NN)


def low_quarter(across):
    core, yh = lax.axis_index("core"), lax.axis_index("yh")
    return jnp.bitwise_xor(jnp.bitwise_xor(core, yh), across)


def call(kernel, name, in_specs, out_specs, out_shape, scratch, limit, flops, **more):
    return pl.pallas_call(
        kernel,
        in_specs=in_specs,
        out_specs=out_specs,
        out_shape=out_shape,
        scratch_shapes=scratch,
        compiler_params=pltpu.CompilerParams(vmem_limit_bytes=limit << 20),
        cost_estimate=pl.CostEstimate(flops=flops, transcendentals=0, bytes_accessed=10 << 20),
        name=name,
        **more,
    )


def source_kernel(order, residual, counts, *refs):
    outs, residual_buffer, counts_buffer, sems = refs[:-3], *refs[-3:]
    me = lax.axis_index(NARROW)
    steps = [(i, part) for i in range(len(order)) for part in range(2)]

    def copies(step):
        i, part = step
        kept = jnp.bitwise_xor(lax.axis_index("yl"), part)
        planes = pl.ds(4 * jnp.bitwise_xor(me, order[i]) + 2 * kept, 2)
        slot = 2 * i + part
        yield pltpu.make_async_copy(residual.at[planes], residual_buffer.at[slot], sems.at[0, slot])
        yield pltpu.make_async_copy(counts.at[planes], counts_buffer.at[slot], sems.at[1, slot])

    for step in steps:
        for copy in copies(step):
            copy.start()
    for step in steps:
        for copy in copies(step):
            copy.wait()
        i, part = step
        slot = 2 * i + part
        value = residual_buffer[slot] + 0.3 * (counts_buffer[slot].astype(F32) - 2.0)
        outs[i][part * 128 : (part + 1) * 128] = value.reshape(128, 512)


def make_source(order, residual, counts):
    def kernel(*refs):
        source_kernel(order, *refs)

    count = len(order)
    return call(
        kernel,
        "make_source",
        [HBM] * 2,
        [VMEM] * count,
        [jax.ShapeDtypeStruct((ROWS, 512), F32)] * count,
        [
            pltpu.VMEM((2 * count, 2, 64, 512), F32),
            pltpu.VMEM((2 * count, 2, 64, 512), jnp.int32),
            pltpu.SemaphoreType.DMA((2, 2 * count)),
        ],
        SOURCE_LIMIT,
        1 << 20,
    )(residual, counts)


def prepare_kernel(*refs):
    matrices, outs, buffer, sems = refs[:2], refs[2:6], *refs[6:]
    steps = [(m, r) for m in range(2) for r in range(4)]

    def fetch(index):
        matrix, rows = steps[index]
        source = matrices[matrix].at[pl.ds(rows * TILE, TILE)]
        return pltpu.make_async_copy(source, buffer.at[index % 4], sems.at[index % 4])

    for index in range(3):
        fetch(index).start()
    for index, (matrix, rows) in enumerate(steps):
        if index + 3 < 8:
            fetch(index + 3).start()
        fetch(index).wait()
        high, low = split(buffer[index % 4])
        outs[2 * matrix][rows * TILE : (rows + 1) * TILE] = high
        outs[2 * matrix + 1][rows * TILE : (rows + 1) * TILE] = low


def prepare(*matrices):
    return call(
        prepare_kernel,
        "prepare",
        [HBM] * 2,
        [VMEM] * 4,
        [jax.ShapeDtypeStruct((HALF, HALF), BF16)] * 4,
        [pltpu.VMEM((4, TILE, HALF), F32), pltpu.SemaphoreType.DMA((4,))],
        PREPARE_LIMIT,
        2 << 30,
    )(*matrices)


def send(block, d, cores=(0, 1)):
    pairs = [(n, n ^ d) for n in range(8) if n // 2 % 2 in cores]
    return lax.ppermute(block, PLACES, pairs)


def forward_y_kernel(across, near_ref, first, second, eh, el, oh, ol, _, *refs):
    held, out_ref, halves = refs[:-2], refs[-2], refs[-1]
    yh, yl = lax.axis_index("yh"), lax.axis_index("yl")
    here, there = (pl.ds(pl.multiple_of(128 * v, 128), 128) for v in (yl, 1 - yl))
    near_rows = pl.ds(128 * across, 128)
    far_rows = pl.ds(128 * (1 - across), 128)
    halves[yh, here] = near_ref[0:128]
    for core, ways in enumerate((first, second)):

        @pl.when(lax.axis_index("core") == core)
        def _(ways=ways):
            halves[yh, there] = ways[0][near_rows]
            halves[1 - yh, here] = ways[1][far_rows]
            halves[1 - yh, there] = ways[2][far_rows]

    flipper = mirror()
    sym, anti = [], []
    for part in range(2):
        low = halves[0, :, part * TILE : (part + 1) * TILE]
        high = flip_lanes(halves[1, :, (1 - part) * TILE : (2 - part) * TILE], flipper)
        sym.append(split(low + high))
        anti.append(split(low - high))
    rows = pl.ds(pl.multiple_of(512 * low_quarter(across), 512), 512)
    for base, sides, high, low in ((0, sym, eh, el), (4, anti, oh, ol)):
        left = tuple(jnp.concatenate([s[i] for s in sides], 1) for i in range(2))
        for block in range(4):
            lanes = slice(block * TILE, (block + 1) * TILE)
            result = product(left, (high[rows, lanes], low[rows, lanes]), NN)
            for half in range(2):
                for plane in range(2):
                    start = 128 * half + 64 * plane
                    piece = result[start : start + 64]
                    if held:
                        piece = piece + held[0][plane, base + block, half]
                    out_ref[plane, base + block, half] = piece


def forward_y(across, near, first, second, matrices, token, held):
    def kernel(near_ref, *refs):
        forward_y_kernel(across, near_ref, refs[:3], refs[3:6], *refs[6:])

    more = [] if held is None else [held]
    return call(
        kernel,
        "forward_y",
        [VMEM] * (12 + len(more)),
        VMEM,
        jax.ShapeDtypeStruct((2, 8, 2, 64, TILE), F32),
        [pltpu.VMEM((2, ROWS, 512), F32)],
        KERNEL_LIMIT,
        2 << 30,
    )(near, *first, *second, *matrices, token, *more)


def pieces(value):
    high = value.astype(BF16)
    rest = value - high.astype(F32)
    middle = rest.astype(BF16)
    low = (rest - middle.astype(F32)).astype(BF16)
    return [high.astype(F32), middle.astype(F32), low.astype(F32)]


def inverse_kernel(lamz_ref, lamy_ref, screen_ref, out_ref):
    place = lax.axis_index(WIDE)
    plane = 4 * lax.axis_index(NARROW) + 2 * lax.axis_index("yl") + place // 8
    modes = place % 8
    shift = jnp.concatenate([lamy_ref[pl.ds(2 * modes + i, 1)] for i in range(2)], 1)
    shift = pieces(shift + screen_ref[plane])
    shift = jnp.concatenate(shift + [jnp.ones((1, TILE), F32)] * 3, 0).astype(BF16)
    for parity in range(2):
        lam = jnp.concatenate([lamz_ref[8 * parity + i : 8 * parity + i + 1] for i in range(8)], 1)
        lam = jnp.concatenate([jnp.ones((1, HALF), F32)] * 3 + pieces(lam), 0).astype(BF16)
        out_ref[parity] = 1.0 / dot(lam, shift, TN)


def inverse(lam_z, lam_y, screening):
    return call(
        inverse_kernel,
        "inverse",
        [VMEM] * 2 + [pl.BlockSpec(memory_space=pltpu.SMEM)],
        VMEM,
        jax.ShapeDtypeStruct((2, HALF, TILE), F32),
        [],
        8,
        1 << 30,
    )(lam_z.reshape(16, LANES), lam_y.reshape(16, LANES), screening)


def z_rows(block):
    z, yl = divmod(block, 2)
    return slice(4 * z, 4 * z + 4), yl


def solve_z_kernel(x_ref, eh, el, oh, ol, inverse_ref, out_ref, scaled):
    flipper = mirror()
    sym, anti = [], []
    for block in range(4):
        low = x_ref[z_rows(block)].reshape(TILE, TILE)
        high = x_ref[z_rows(7 - block)].reshape(TILE, TILE)
        high = flip_rows(high, flipper)
        sym.append(split(low + high))
        anti.append(split(low - high))
    for parity, sides, matrix in ((0, sym, (eh, el)), (1, anti, (oh, ol))):
        right = tuple(jnp.concatenate([s[i] for s in sides], 0) for i in range(2))
        for block in range(4):
            part = slice(block * TILE, (block + 1) * TILE)
            spectral = product((matrix[0][:, part], matrix[1][:, part]), right, TN)
            pair = split(spectral * inverse_ref[parity, part])
            scaled[parity, 0, part], scaled[parity, 1, part] = pair
    for block in range(4):
        rows = slice(block * TILE, (block + 1) * TILE)
        even = product((eh[rows], el[rows]), (scaled[0, 0], scaled[0, 1]), NN)
        odd = product((oh[rows], ol[rows]), (scaled[1, 0], scaled[1, 1]), NN)
        out_ref[z_rows(block)] = (even + odd).reshape(4, 64, TILE)
        flipped = flip_rows(even - odd, flipper)
        out_ref[z_rows(7 - block)] = flipped.reshape(4, 64, TILE)


def solve_z(x, matrices, weights):
    return call(
        solve_z_kernel,
        "solve_z",
        [VMEM] * 6,
        VMEM,
        jax.ShapeDtypeStruct((16, 2, 64, TILE), F32),
        [pltpu.VMEM((2, 2, HALF, TILE), BF16)],
        KERNEL_LIMIT,
        6 << 30,
    )(x, *matrices, weights)


def backward_y_kernel(across, x_ref, eh, el, oh, ol, near_ref, far_ref, halves):
    flipper = mirror()
    sides = []
    for parity in range(2):
        blocks = [x_ref[:, 4 * parity + i].reshape(ROWS, TILE) for i in range(4)]
        sides.append(split(jnp.concatenate(blocks, 1)))
    start = 512 * low_quarter(across)

    def keep(side, part, value):
        lanes = slice(part * TILE, (part + 1) * TILE)
        for plane in range(2):
            for half in range(2):
                rows = 128 * plane + 64 * half
                target = slice(64 * plane, 64 * plane + 64)
                halves[side, half, target, lanes] = value[rows : rows + 64]

    for part in range(2):
        rows = pl.ds(pl.multiple_of(start + part * TILE, TILE), TILE)
        even = product(sides[0], (eh[rows], el[rows]), NT)
        odd = product(sides[1], (oh[rows], ol[rows]), NT)
        keep(0, part, even + odd)
        keep(1, 1 - part, flip_lanes(even - odd, flipper))
    yh, yl = lax.axis_index("yh"), lax.axis_index("yl")
    for side, ref in ((yh, near_ref), (1 - yh, far_ref)):
        ref[0:128] = halves[side, yl]
        ref[128:256] = halves[side, 1 - yl]


def backward_y(across, x, matrices):
    def kernel(*refs):
        backward_y_kernel(across, *refs)

    return call(
        kernel,
        "backward_y",
        [VMEM] * 5,
        [VMEM] * 2,
        [jax.ShapeDtypeStruct((ROWS, 512), F32)] * 2,
        [pltpu.VMEM((2, 2, 128, 512), F32)],
        KERNEL_LIMIT,
        2 << 30,
    )(x, *matrices)


def place_kernel(where, *refs):
    out, sems = refs[-2], refs[-1]
    me, yl = lax.axis_index(NARROW), lax.axis_index("yl")

    def copy(index):
        d, half, array, row = where[index]
        start = ROWS * jnp.bitwise_xor(me, d) + 128 * jnp.bitwise_xor(yl, half)
        target = out.at[pl.ds(pl.multiple_of(start, 128), 128)]
        source = refs[array].at[pl.ds(row, 128)]
        return pltpu.make_async_copy(source, target, sems.at[index])

    for index in range(len(where)):
        copy(index).start()
    for index in range(len(where)):
        copy(index).wait()


def place(where, blocks, held):
    def kernel(*refs):
        place_kernel(where, *refs)

    more = [] if held is None else [held]
    return call(
        kernel,
        "place",
        [pl.BlockSpec(memory_space=pl.ANY)] * len(blocks) + [HBM] * len(more),
        HBM,
        jax.ShapeDtypeStruct((HALF, 512), F32),
        [pltpu.SemaphoreType.DMA((len(where),))],
        2,
        1 << 20,
        input_output_aliases={} if held is None else {len(blocks): 0},
    )(*blocks, *more)


def on_device(residual, counts, screening, even_y, odd_y, even_z, odd_z, lam_y, lam_z):
    block3, block2 = make_source((3, 2), residual, counts)
    block1, block0 = make_source((1, 0), residual, counts)
    block3, block1 = send(block3, 2), send(block1, 2)
    ways = [
        jnp.concatenate([block0[128:], block1[128:]]),
        jnp.concatenate([block2[:128], block3[:128]]),
        jnp.concatenate([block2[128:], block3[128:]]),
    ]
    first = [send(way, d, (0,)) for way, d in zip(ways, (1, 4, 5))]
    matrix_y, matrix_z = prepare(even_y, odd_y), prepare(even_z, odd_z)
    weights = inverse(lam_z, lam_y, screening)
    first, block1 = lax.optimization_barrier((first, block1))
    token = send(first[1][:8, :LANES], 2, (0,))
    ways, token = lax.optimization_barrier((ways, token))
    second = [send(way, d, (1,)) for way, d in zip(ways, (1, 4, 5))]
    block0, block1, matrix_y, matrix_z, weights = lax.optimization_barrier(
        (block0, block1, matrix_y, matrix_z, weights)
    )
    along = forward_y(1, block1, first, second, matrix_y, token, None)
    along = forward_y(0, block0, first, second, matrix_y, token, along)
    columns = lax.all_to_all(along.reshape(16, 2, 64, TILE), WIDE, 0, 0, tiled=True)
    back = solve_z(columns, matrix_z, weights)
    rows = lax.all_to_all(back, WIDE, 0, 0, tiled=True).reshape(2, 8, 2, 64, TILE)
    block1, block2 = backward_y(1, rows, matrix_y)
    block0, block3 = backward_y(0, rows, matrix_y)
    far = send(jnp.concatenate([block2[:128], block3[:128]]), 4)
    across = send(jnp.concatenate([block2[128:], block3[128:]]), 5)
    near = send(jnp.concatenate([block0[128:], block1[128:]]), 1)
    early, far, near = lax.optimization_barrier((block1[:128], far, near))
    early = send(jnp.concatenate([early, near[128:], far[128:]]), 2)
    late = send(across[128:], 2)
    out = place(
        ((0, 0, 0, 0), (0, 1, 1, 0), (2, 0, 2, 0), (2, 1, 3, 0)),
        (block0, near, far, across),
        None,
    )
    where = ((1, 0, 0, 0), (1, 1, 0, 128), (3, 0, 0, 256), (3, 1, 1, 0))
    out = place(where, (early, late), out)
    return out.reshape(16, 64, 512)


def solution(mesh):
    fine = Mesh(mesh.devices.reshape(2, 2, 4, 2, 4), ("yh", "core", "z", "yl", "x"))
    split_spec = P(None, ("z", "yl", "x"), NARROW)
    return jax.shard_map(
        on_device,
        mesh=fine,
        in_specs=(split_spec, split_spec) + (P(),) * 7,
        out_specs=split_spec,
        check_vma=False,
    )
```

time: 134 us -> 133 us (level)
  waiting for transfers between devices: 30.7 us -> 38 us
  blocking collectives: 52.3 us -> 45.4 us
  Pallas kernels: 29.8 us -> 27 us
  local copies, waits for them, and re-layouts: 0.04 us -> 2.05 us
    ppermute x11 -> x14, waiting for transfers between devices: 30.7 us -> 38 us  [send(): return lax.ppermute(block, PLACES, pairs)]
    all_to_all x2, blocking collectives: 52.3 us -> 45.4 us  [the longest x1 25.2 us: on_device(): lax.all_to_all(along.reshape(16, 2, 64, TILE), WIDE, 0, 0, tiled=True)]
    pallas_call x5 -> x6, Pallas kernels: 17.7 us -> 15.6 us  [the longest x1 8.27 us: solve_z(): call(solve_z_kernel, 'solve_z', [VMEM] * 6, VMEM, jax.ShapeDtypeStruct((1...]
    unnamed x14, local copies, waits for them, and re-layouts: 0.04 us -> 1.75 us
    ppermute x11 -> x14, starting transfers between devices: 20.1 us -> 19.2 us  [send(): return lax.ppermute(block, PLACES, pairs)]
  transfers between devices with their start and end apart: 11 -> 14, of which waited for: 6 -> 6; matrix products, arithmetic and copies ran while one was open for 0% -> 0% of each run, Pallas kernels for 8% -> 5%
where the time goes in v4:
time: 133 us
  blocking collectives  45.4 us (34%)
  waiting for transfers between devices  38 us (29%)
  Pallas kernels  27 us (20%)
  starting transfers between devices  19.2 us (14%)
  local copies, waits for them, and re-layouts  2.05 us (2%)
    ppermute x14, waiting for transfers between devices, send(): return lax.ppermute(block, PLACES, pairs)  38 us
    all_to_all x1, blocking collectives, on_device(): lax.all_to_all(along.reshape(16, 2, 64, TILE), WIDE, 0, 0, tiled=True)  25.2 us
    all_to_all x1, blocking collectives, on_device(): lax.all_to_all(back, WIDE, 0, 0, tiled=True).reshape(2, 8, 2, 64, TILE)  20.2 us
    ppermute x14, starting transfers between devices, send(): return lax.ppermute(block, PLACES, pairs)  19.2 us
    pallas_call x1, Pallas kernels, solve_z(): call(solve_z_kernel, 'solve_z', [VMEM] * 6, VMEM, jax.ShapeDtypeStruct((1...  8.27 us
    pallas_call x2, Pallas kernels, backward_y(): call(kernel, 'backward_y', [VMEM] * 5, [VMEM] * 2, [jax.ShapeDtypeStruct(...  4.74 us
    pallas_call x2, Pallas kernels, forward_y(): call(kernel, 'forward_y', [VMEM] * (12 + len(more)), VMEM, jax.ShapeDtype...  4.3 us
    pallas_call x2, Pallas kernels, prepare(): call(prepare_kernel, 'prepare', [HBM] * 2, [VMEM] * 4, [jax.ShapeDtypeStr...  3.45 us
  transfers between devices with their start and end apart: 14, of which 6 were waited for; matrix products, arithmetic and copies ran while one was open for 0% of the time, Pallas kernels for 5%

profile of v4, /device:TPU:1, one launch (start us, length us, event | category | flops | bytes accessed | tf_op | source)
XLA Modules:
  0.0 132.5 jit_solution(13514785939016377982)
XLA Ops:
  0.0 1.6 %make_source.3 = (f32[256,512]{1,0:T(8,128)S(1)}, f32[256,512]{1,0:T(8,128)S(1)}) custom-call(f32[16,64,512]{2,1,0:T(8,128)} %refs_0_.5, s32[16,64,512]{2,1,0:T(8,128)} %refs_1_.5), custom_call_target="tpu_custom_call" | custom-call | flops 1048576 | bytes 10485760 | tf_op jit(solution)/shard_map/make_source/pallas_call | solution.py:110
  1.6 1.5 %collective-permute-start.2 = (f32[256,512]{1,0:T(8,128)S(1)}, f32[256,512]{1,0:T(8,128)S(1)}, u32[]{:S(2)}, u32[]{:S(2)}) collective-permute-start(f32[256,512]{1,0:T(8,128)S(1)} %get-tuple-element.46), channel_id=1, source_target_pairs={{0,32},{4,36},{32,0},{36,4},{64,96},{68,100},{96,64},{100,68},{1,3... | collective-permute-start | bytes 1572872 | tf_op jit(solution)/shard_map/ppermute | solution.py:161
  3.1 1.6 %make_source.2 = (f32[256,512]{1,0:T(8,128)S(1)}, f32[256,512]{1,0:T(8,128)S(1)}) custom-call(f32[16,64,512]{2,1,0:T(8,128)} %refs_0_.5, s32[16,64,512]{2,1,0:T(8,128)} %refs_1_.5), custom_call_target="tpu_custom_call" | custom-call | flops 1048576 | bytes 10485760 | tf_op jit(solution)/shard_map/make_source/pallas_call | solution.py:110
  7.7 1.4 %collective-permute-start.5 = (f32[8,128]{1,0:T(8,128)S(1)}, f32[8,128]{1,0:T(8,128)S(1)}, u32[]{:S(2)}, u32[]{:S(2)}) collective-permute-start(f32[8,128]{1,0:T(8,128)S(1)} %slice.57), channel_id=1, source_target_pairs={{0,32},{4,36},{64,96},{68,100},{1,33},{5,37},{65,97},{69,101},{2,3... | collective-permute-start | bytes 12296 | tf_op jit(solution)/shard_map/ppermute | solution.py:161
  9.2 18.2 %collective-permute-done.5.refs_10_ = f32[8,128]{1,0:T(8,128)S(1)} collective-permute-done((f32[8,128]{1,0:T(8,128)S(1)}, f32[8,128]{1,0:T(8,128)S(1)}, u32[]{:S(2)}, u32[]{:S(2)}) %collective-permute-start.5) | collective-permute-done | bytes 4128 | tf_op jit(solution)/shard_map/ppermute | solution.py:161
  27.4 2.0 %collective-permute-start.6 = (f32[256,512]{1,0:T(8,128)S(1)}, f32[256,512]{1,0:T(8,128)S(1)}, u32[]{:S(2)}, u32[]{:S(2)}) collective-permute-start(f32[256,512]{1,0:T(8,128)S(1)} %pad_maximum_fusion.1), channel_id=1, source_target_pairs={{32,36},{36,32},{96,100},{100,96},{33,37},{37,33},{97,101},{101,97... | collective-permute-start | bytes 1572872 | tf_op jit(solution)/shard_map/ppermute | solution.py:161
  29.4 4.9 %collective-permute-start.7 = (f32[256,512]{1,0:T(8,128)S(1)}, f32[256,512]{1,0:T(8,128)S(1)}, u32[]{:S(2)}, u32[]{:S(2)}) collective-permute-start(f32[256,512]{1,0:T(8,128)S(1)} %pad_maximum_fusion.2), channel_id=1, source_target_pairs={{32,96},{36,100},{96,32},{100,36},{33,97},{37,101},{97,33},{101,37... | collective-permute-start | bytes 1572872 | tf_op jit(solution)/shard_map/ppermute | solution.py:161
  34.3 2.7 %collective-permute-start.8 = (f32[256,512]{1,0:T(8,128)S(1)}, f32[256,512]{1,0:T(8,128)S(1)}, u32[]{:S(2)}, u32[]{:S(2)}) collective-permute-start(f32[256,512]{1,0:T(8,128)S(1)} %pad_maximum_fusion.3), channel_id=1, source_target_pairs={{32,100},{36,96},{96,36},{100,32},{33,101},{37,97},{97,37},{101,33... | collective-permute-start | bytes 1572872 | tf_op jit(solution)/shard_map/ppermute | solution.py:161
  38.1 1.7 %prepare.2 = (bf16[1024,1024]{1,0:T(8,128)(2,1)S(1)}, bf16[1024,1024]{1,0:T(8,128)(2,1)S(1)}, bf16[1024,1024]{1,0:T(8,128)(2,1)S(1)}, bf16[1024,1024]{1,0:T(8,128)(2,1)S(1)}) custom-call(f32[1024,1024]{1,0:T(8,128)S(1)} %copy-done, f32[1024,1024]{1,0:T(8,128)S(1)} %copy-done.1), custom_call_target="tpu_custom_call" | custom-call | flops 2147483648 | bytes 10485760 | tf_op jit(solution)/shard_map/prepare/pallas_call | solution.py:147
  40.2 1.3 copy-done.3
  41.5 1.7 %prepare.3 = (bf16[1024,1024]{1,0:T(8,128)(2,1)S(1)}, bf16[1024,1024]{1,0:T(8,128)(2,1)S(1)}, bf16[1024,1024]{1,0:T(8,128)(2,1)S(1)}, bf16[1024,1024]{1,0:T(8,128)(2,1)S(1)}) custom-call(f32[1024,1024]{1,0:T(8,128)S(1)} %copy-done.2, f32[1024,1024]{1,0:T(8,128)S(1)} %copy-done.3), custom_call_target="tpu_custom_call" | custom-call | flops 2147483648 | bytes 10485760 | tf_op jit(solution)/shard_map/prepare/pallas_call | solution.py:147
  43.3 1.4 %collective-permute-done.7.refs_4_ = f32[256,512]{1,0:T(8,128)S(1)} collective-permute-done((f32[256,512]{1,0:T(8,128)S(1)}, f32[256,512]{1,0:T(8,128)S(1)}, u32[]{:S(2)}, u32[]{:S(2)}) %collective-permute-start.7) | collective-permute-done | bytes 524320 | tf_op jit(solution)/shard_map/ppermute | solution.py:161
  44.6 5.5 %collective-permute-done.8.refs_5_ = f32[256,512]{1,0:T(8,128)S(1)} collective-permute-done((f32[256,512]{1,0:T(8,128)S(1)}, f32[256,512]{1,0:T(8,128)S(1)}, u32[]{:S(2)}, u32[]{:S(2)}) %collective-permute-start.8) | collective-permute-done | bytes 524320 | tf_op jit(solution)/shard_map/ppermute | solution.py:161
  50.1 2.1 %forward_y.2.refs_11_ = f32[2,8,2,64,256]{4,3,2,1,0:T(8,128)S(1)} custom-call(f32[256,512]{1,0:T(8,128)S(1)} %collective-permute-done.near_ref, f32[256,512]{1,0:T(8,128)S(1)} %collective-permute-done.1.refs_0_, f32[256,512]{1,0:T(8,128)S(1)} %collective-permute-done.3.refs_1_, f32[256,512]{1,0:T(8,128)S(1)} %collective-permute-done.4.refs_2_, ...), custom_call_target="tpu_custom_call" | custom-call | flops 2147483648 | bytes 10485760 | tf_op jit(solution)/shard_map/forward_y/pallas_call | solution.py:206
  52.3 2.2 %forward_y.3 = f32[2,8,2,64,256]{4,3,2,1,0:T(8,128)S(1)} custom-call(f32[256,512]{1,0:T(8,128)S(1)} %get-tuple-element.56.near_ref, f32[256,512]{1,0:T(8,128)S(1)} %collective-permute-done.1.refs_0_, f32[256,512]{1,0:T(8,128)S(1)} %collective-permute-done.3.refs_1_, f32[256,512]{1,0:T(8,128)S(1)} %collective-permute-done.4.refs_2_, ...), custom_call_target="tpu_custom_call" | custom-call | flops 2147483648 | bytes 10485760 | tf_op jit(solution)/shard_map/forward_y/pallas_call | solution.py:206
  54.4 25.2 %all_to_all.10.x_ref = f32[16,2,64,256]{3,2,1,0:T(8,128)S(1)} all-to-all(f32[16,2,64,256]{3,2,1,0:T(8,128)S(1)} %bitcast.7), channel_id=1, replica_groups=mesh['yh'=2,'core'=2,'z'=4,'yl'=2,'x'=4] {'z','x'}, dimensions={0} | all-to-all | bytes 4194304 | tf_op jit(solution)/shard_map/all_to_all | solution.py:395
  79.7 8.3 %solve_z.1 = f32[16,2,64,256]{3,2,1,0:T(8,128)S(1)} custom-call(f32[16,2,64,256]{3,2,1,0:T(8,128)S(1)} %all_to_all.10.x_ref, bf16[1024,1024]{1,0:T(8,128)(2,1)S(1)} %get-tuple-element.69.eh, bf16[1024,1024]{1,0:T(8,128)(2,1)S(1)} %get-tuple-element.70.el, bf16[1024,1024]{1,0:T(8,128)(2,1)S(1)} %get-tuple-element.71.oh, ...), custom_call_target="tpu_custom_call" | custom-call | flops 6442450944 | bytes 10485760 | tf_op jit(solution)/shard_map/solve_z/pallas_call | solution.py:283
  87.9 20.2 %all_to_all.11 = f32[16,2,64,256]{3,2,1,0:T(8,128)S(1)} all-to-all(f32[16,2,64,256]{3,2,1,0:T(8,128)S(1)} %solve_z.1), channel_id=1, replica_groups=mesh['yh'=2,'core'=2,'z'=4,'yl'=2,'x'=4] {'z','x'}, dimensions={0} | all-to-all | bytes 4194304 | tf_op jit(solution)/shard_map/all_to_all | solution.py:397
  108.1 2.4 %backward_y.3 = (f32[256,512]{1,0:T(8,128)S(1)}, f32[256,512]{1,0:T(8,128)S(1)}) custom-call(f32[2,8,2,64,256]{4,3,2,1,0:T(8,128)S(1)} %bitcast.5, bf16[1024,1024]{1,0:T(8,128)(2,1)S(1)} %get-tuple-element.63.refs_6_.refs_1_, bf16[1024,1024]{1,0:T(8,128)(2,1)S(1)} %get-tuple-element.64.refs_7_.refs_2_, ...), custom_call_target="tpu_custom_call" | custom-call | flops 2147483648 | bytes 10485760 | tf_op jit(solution)/shard_map/backward_y/pallas_call | solution.py:327
  110.5 2.4 %backward_y.2 = (f32[256,512]{1,0:T(8,128)S(1)}, f32[256,512]{1,0:T(8,128)S(1)}) custom-call(f32[2,8,2,64,256]{4,3,2,1,0:T(8,128)S(1)} %bitcast.6, bf16[1024,1024]{1,0:T(8,128)(2,1)S(1)} %get-tuple-element.63.refs_6_.refs_1_, bf16[1024,1024]{1,0:T(8,128)(2,1)S(1)} %get-tuple-element.64.refs_7_.refs_2_, ...), custom_call_target="tpu_custom_call" | custom-call | flops 2147483648 | bytes 10485760 | tf_op jit(solution)/shard_map/backward_y/pallas_call | solution.py:327
  113.7 1.1 collective-permute-start.10
  114.8 1.8 %collective-permute-start.12 = (f32[256,512]{1,0:T(8,128)S(1)}, f32[256,512]{1,0:T(8,128)S(1)}, u32[]{:S(2)}, u32[]{:S(2)}) collective-permute-start(f32[256,512]{1,0:T(8,128)S(1)} %pad_maximum_fusion.6), channel_id=1, source_target_pairs={{0,68},{4,64},{32,100},{36,96},{64,4},{68,0},{96,36},{100,32},{1,6... | collective-permute-start | bytes 1572872 | tf_op jit(solution)/shard_map/ppermute | solution.py:161
  116.7 6.3 %collective-permute-done.9.refs_2_ = f32[256,512]{1,0:T(8,128)S(1)} collective-permute-done((f32[256,512]{1,0:T(8,128)S(1)}, f32[256,512]{1,0:T(8,128)S(1)}, u32[]{:S(2)}, u32[]{:S(2)}) %collective-permute-start.9) | collective-permute-done | bytes 524320 | tf_op jit(solution)/shard_map/ppermute | solution.py:161
  123.0 5.5 %collective-permute-done.10.refs_1_ = f32[256,512]{1,0:T(8,128)S(1)} collective-permute-done((f32[256,512]{1,0:T(8,128)S(1)}, f32[256,512]{1,0:T(8,128)S(1)}, u32[]{:S(2)}, u32[]{:S(2)}) %collective-permute-start.10) | collective-permute-done | bytes 524320 | tf_op jit(solution)/shard_map/ppermute | solution.py:161
  (51 shorter events, 9.0 us)
Async XLA Ops:
  1.6 3.3 %collective-permute-start.2 = (f32[256,512]{1,0:T(8,128)S(1)}, f32[256,512]{1,0:T(8,128)S(1)}, u32[]{:S(2)}, u32[]{:S(2)}) collective-permute-start(f32[256,512]{1,0:T(8,128)S(1)} %get-tuple-element.46), channel_id=1, source_target_pairs={{0,32},{4,36},{32,0},{36,4},{64,96},{68,100},{96,64},{100,68},{1,3... | collective-permute-start | bytes 1572872 | tf_op jit(solution)/shard_map/ppermute | solution.py:161
  4.7 2.0 %collective-permute-start = (f32[256,512]{1,0:T(8,128)S(1)}, f32[256,512]{1,0:T(8,128)S(1)}, u32[]{:S(2)}, u32[]{:S(2)}) collective-permute-start(f32[256,512]{1,0:T(8,128)S(1)} %get-tuple-element.44), channel_id=1, source_target_pairs={{0,32},{4,36},{32,0},{36,4},{64,96},{68,100},{96,64},{100,68},{1,3... | collective-permute-start | bytes 1572872 | tf_op jit(solution)/shard_map/ppermute | solution.py:161
  4.9 33.1 %copy-start.1 = (f32[1024,1024]{1,0:T(8,128)S(1)}, f32[1024,1024]{1,0:T(8,128)}, u32[]{:S(2)}) copy-start(f32[1024,1024]{1,0:T(8,128)} %refs_1_.6) | copy-start | bytes 12582916
  5.0 32.0 %copy-start.4 = (f32[2048]{0:T(1024)S(1)}, f32[2048]{0:T(1024)}, u32[]{:S(2)}) copy-start(f32[2048]{0:T(1024)} %param.17) | copy-start | bytes 24580
  5.0 32.0 %copy-start.5 = (f32[2048]{0:T(1024)S(1)}, f32[2048]{0:T(1024)}, u32[]{:S(2)}) copy-start(f32[2048]{0:T(1024)} %param.16) | copy-start | bytes 24580
  5.0 32.0 %copy-start.6 = (f32[16]{0:T(128)S(1)}, f32[16]{0:T(128)}, u32[]{:S(2)}) copy-start(f32[16]{0:T(128)} %screen_ref.1) | copy-start | bytes 196
  5.1 2.6 %collective-permute-start.3 = (f32[256,512]{1,0:T(8,128)S(1)}, f32[256,512]{1,0:T(8,128)S(1)}, u32[]{:S(2)}, u32[]{:S(2)}) collective-permute-start(f32[256,512]{1,0:T(8,128)S(1)} %pad_maximum_fusion.2), channel_id=1, source_target_pairs={{0,64},{4,68},{64,0},{68,4},{1,65},{5,69},{65,1},{69,5},{2,66},{6,... | collective-permute-start | bytes 1572872 | tf_op jit(solution)/shard_map/ppermute | solution.py:161
  5.9 1.8 %collective-permute-start.4 = (f32[256,512]{1,0:T(8,128)S(1)}, f32[256,512]{1,0:T(8,128)S(1)}, u32[]{:S(2)}, u32[]{:S(2)}) collective-permute-start(f32[256,512]{1,0:T(8,128)S(1)} %pad_maximum_fusion.3), channel_id=1, source_target_pairs={{0,68},{4,64},{64,4},{68,0},{1,69},{5,65},{65,5},{69,1},{2,70},{6,... | collective-permute-start | bytes 1572872 | tf_op jit(solution)/shard_map/ppermute | solution.py:161
  6.8 31.2 %copy-start = (f32[1024,1024]{1,0:T(8,128)S(1)}, f32[1024,1024]{1,0:T(8,128)}, u32[]{:S(2)}) copy-start(f32[1024,1024]{1,0:T(8,128)} %refs_0_.6) | copy-start | bytes 12582916
  6.9 0.9 collective-permute-start.1
  7.7 19.6 %collective-permute-start.5 = (f32[8,128]{1,0:T(8,128)S(1)}, f32[8,128]{1,0:T(8,128)S(1)}, u32[]{:S(2)}, u32[]{:S(2)}) collective-permute-start(f32[8,128]{1,0:T(8,128)S(1)} %slice.57), channel_id=1, source_target_pairs={{0,32},{4,36},{64,96},{68,100},{1,33},{5,37},{65,97},{69,101},{2,3... | collective-permute-start | bytes 12296 | tf_op jit(solution)/shard_map/ppermute | solution.py:161
  27.4 15.9 %collective-permute-start.6 = (f32[256,512]{1,0:T(8,128)S(1)}, f32[256,512]{1,0:T(8,128)S(1)}, u32[]{:S(2)}, u32[]{:S(2)}) collective-permute-start(f32[256,512]{1,0:T(8,128)S(1)} %pad_maximum_fusion.1), channel_id=1, source_target_pairs={{32,36},{36,32},{96,100},{100,96},{33,37},{37,33},{97,101},{101,97... | collective-permute-start | bytes 1572872 | tf_op jit(solution)/shard_map/ppermute | solution.py:161
  29.4 15.3 %collective-permute-start.7 = (f32[256,512]{1,0:T(8,128)S(1)}, f32[256,512]{1,0:T(8,128)S(1)}, u32[]{:S(2)}, u32[]{:S(2)}) collective-permute-start(f32[256,512]{1,0:T(8,128)S(1)} %pad_maximum_fusion.2), channel_id=1, source_target_pairs={{32,96},{36,100},{96,32},{100,36},{33,97},{37,101},{97,33},{101,37... | collective-permute-start | bytes 1572872 | tf_op jit(solution)/shard_map/ppermute | solution.py:161
  34.3 15.9 %collective-permute-start.8 = (f32[256,512]{1,0:T(8,128)S(1)}, f32[256,512]{1,0:T(8,128)S(1)}, u32[]{:S(2)}, u32[]{:S(2)}) collective-permute-start(f32[256,512]{1,0:T(8,128)S(1)} %pad_maximum_fusion.3), channel_id=1, source_target_pairs={{32,100},{36,96},{96,36},{100,32},{33,101},{37,97},{97,37},{101,33... | collective-permute-start | bytes 1572872 | tf_op jit(solution)/shard_map/ppermute | solution.py:161
  38.1 2.2 %copy-start.2 = (f32[1024,1024]{1,0:T(8,128)S(1)}, f32[1024,1024]{1,0:T(8,128)}, u32[]{:S(2)}) copy-start(f32[1024,1024]{1,0:T(8,128)} %refs_0_.7) | copy-start | bytes 12582916
  38.1 3.5 %copy-start.3 = (f32[1024,1024]{1,0:T(8,128)S(1)}, f32[1024,1024]{1,0:T(8,128)}, u32[]{:S(2)}) copy-start(f32[1024,1024]{1,0:T(8,128)} %refs_1_.7) | copy-start | bytes 12582916
  113.1 9.9 %collective-permute-start.9 = (f32[256,512]{1,0:T(8,128)S(1)}, f32[256,512]{1,0:T(8,128)S(1)}, u32[]{:S(2)}, u32[]{:S(2)}) collective-permute-start(f32[256,512]{1,0:T(8,128)S(1)} %pad_maximum_fusion.4), channel_id=1, source_target_pairs={{0,64},{4,68},{32,96},{36,100},{64,0},{68,4},{96,32},{100,36},{1,6... | collective-permute-start | bytes 1572872 | tf_op jit(solution)/shard_map/ppermute | solution.py:161
  113.7 14.8 %collective-permute-start.10 = (f32[256,512]{1,0:T(8,128)S(1)}, f32[256,512]{1,0:T(8,128)S(1)}, u32[]{:S(2)}, u32[]{:S(2)}) collective-permute-start(f32[256,512]{1,0:T(8,128)S(1)} %pad_maximum_fusion.5), channel_id=1, source_target_pairs={{0,4},{4,0},{32,36},{36,32},{64,68},{68,64},{96,100},{100,96},{1,5... | collective-permute-start | bytes 1572872 | tf_op jit(solution)/shard_map/ppermute | solution.py:161
  114.8 13.9 %collective-permute-start.12 = (f32[256,512]{1,0:T(8,128)S(1)}, f32[256,512]{1,0:T(8,128)S(1)}, u32[]{:S(2)}, u32[]{:S(2)}) collective-permute-start(f32[256,512]{1,0:T(8,128)S(1)} %pad_maximum_fusion.6), channel_id=1, source_target_pairs={{0,68},{4,64},{32,100},{36,96},{64,4},{68,0},{96,36},{100,32},{1,6... | collective-permute-start | bytes 1572872 | tf_op jit(solution)/shard_map/ppermute | solution.py:161
  128.6 2.7 %collective-permute-start.11 = (f32[384,512]{1,0:T(8,128)S(1)}, f32[384,512]{1,0:T(8,128)S(1)}, u32[]{:S(2)}, u32[]{:S(2)}) collective-permute-start(f32[384,512]{1,0:T(8,128)S(1)} %pad_maximum_fusion), channel_id=1, source_target_pairs={{0,32},{4,36},{32,0},{36,4},{64,96},{68,100},{96,64},{100,68},{1,3... | collective-permute-start | bytes 2359304 | tf_op jit(solution)/shard_map/ppermute | solution.py:161
  128.7 2.6 %collective-permute-start.13 = (f32[128,512]{1,0:T(8,128)S(1)}, f32[128,512]{1,0:T(8,128)S(1)}, u32[]{:S(2)}, u32[]{:S(2)}) collective-permute-start(f32[128,512]{1,0:T(8,128)S(1)} %slice.71), channel_id=1, source_target_pairs={{0,32},{4,36},{32,0},{36,4},{64,96},{68,100},{96,64},{100,68},{1,3... | collective-permute-start | bytes 786440 | tf_op jit(solution)/shard_map/ppermute | solution.py:161

commit v5 on v3

--- a/solution.py
+++ b/solution.py
@@ -212,13 +212,33 @@
     return [high.astype(F32), middle.astype(F32), low.astype(F32)]
 
 
-def solve_z_kernel(x_ref, eh, el, oh, ol, lamz_ref, lamy_ref, screen_ref, out_ref):
-    flipper = mirror()
+def inverse_kernel(lamz_ref, lamy_ref, screen_ref, out_ref):
     place = lax.axis_index(WIDE)
     plane, modes = 4 * lax.axis_index(NARROW) + place // 8, place % 8
     shift = jnp.concatenate([lamy_ref[pl.ds(2 * modes + i, 1)] for i in range(2)], 1)
     shift = pieces(shift + screen_ref[plane])
     shift = jnp.concatenate(shift + [jnp.ones((1, TILE), F32)] * 3, 0).astype(BF16)
+    for parity in range(2):
+        lam = jnp.concatenate([lamz_ref[8 * parity + i : 8 * parity + i + 1] for i in range(8)], 1)
+        lam = jnp.concatenate([jnp.ones((1, HALF), F32)] * 3 + pieces(lam), 0).astype(BF16)
+        out_ref[parity] = 1.0 / dot(lam, shift, TN)
+
+
+def inverse(lam_z, lam_y, screening):
+    return call(
+        inverse_kernel,
+        "inverse",
+        [VMEM] * 2 + [pl.BlockSpec(memory_space=pltpu.SMEM)],
+        VMEM,
+        jax.ShapeDtypeStruct((2, HALF, TILE), F32),
+        [],
+        8,
+        1 << 30,
+    )(lam_z.reshape(16, LANES), lam_y.reshape(16, LANES), screening)
+
+
+def solve_z_kernel(x_ref, eh, el, oh, ol, inverse_ref, out_ref, scaled):
+    flipper = mirror()
     sym, anti = [], []
     for block in range(4):
         low = x_ref[4 * block : 4 * block + 4].reshape(TILE, TILE)
@@ -226,35 +246,33 @@
         high = flip_rows(high, flipper)
         sym.append(split(low + high))
         anti.append(split(low - high))
-    results = []
     for parity, sides, matrix in ((0, sym, (eh, el)), (1, anti, (oh, ol))):
         right = tuple(jnp.concatenate([s[i] for s in sides], 0) for i in range(2))
-        pair = (matrix[0][...], matrix[1][...])
-        spectral = product(pair, right, TN)
-        lam = jnp.concatenate([lamz_ref[8 * parity + i : 8 * parity + i + 1] for i in range(8)], 1)
-        lam = jnp.concatenate([jnp.ones((1, HALF), F32)] * 3 + pieces(lam), 0).astype(BF16)
-        scaled = spectral / dot(lam, shift, TN)
-        results.append(product(pair, split(scaled), NN))
-    total = results[0] + results[1]
-    rest = results[0] - results[1]
+        for block in range(4):
+            part = slice(block * TILE, (block + 1) * TILE)
+            spectral = product((matrix[0][:, part], matrix[1][:, part]), right, TN)
+            pair = split(spectral * inverse_ref[parity, part])
+            scaled[parity, 0, part], scaled[parity, 1, part] = pair
     for block in range(4):
         rows = slice(block * TILE, (block + 1) * TILE)
-        out_ref[4 * block : 4 * block + 4] = total[rows].reshape(4, 64, TILE)
-        flipped = flip_rows(rest[rows], flipper)
+        even = product((eh[rows], el[rows]), (scaled[0, 0], scaled[0, 1]), NN)
+        odd = product((oh[rows], ol[rows]), (scaled[1, 0], scaled[1, 1]), NN)
+        out_ref[4 * block : 4 * block + 4] = (even + odd).reshape(4, 64, TILE)
+        flipped = flip_rows(even - odd, flipper)
         out_ref[28 - 4 * block : 32 - 4 * block] = flipped.reshape(4, 64, TILE)
 
 
-def solve_z(x, matrices, lam_z, lam_y, screening):
+def solve_z(x, matrices, weights):
     return call(
         solve_z_kernel,
         "solve_z",
-        [VMEM] * 7 + [pl.BlockSpec(memory_space=pltpu.SMEM)],
+        [VMEM] * 6,
         VMEM,
         jax.ShapeDtypeStruct((32, 64, TILE), F32),
-        [],
+        [pltpu.VMEM((2, 2, HALF, TILE), BF16)],
         KERNEL_LIMIT,
         6 << 30,
-    )(x, *matrices, lam_z.reshape(16, LANES), lam_y.reshape(16, LANES), screening)
+    )(x, *matrices, weights)
 
 
 def backward_y_kernel(across, x_ref, eh, el, oh, ol, near_ref, far_ref, halves):
@@ -334,8 +352,9 @@
     own0, sibling0 = send(block2, 2, (0,)), send(block3, 2, (0,))
     block1 = send(block1, 1)
     matrix_y, matrix_z = prepare(even_y, odd_y), prepare(even_z, odd_z)
-    block1, sibling0, own0, matrix_y, matrix_z = lax.optimization_barrier(
-        (block1, sibling0, own0, matrix_y, matrix_z)
+    weights = inverse(lam_z, lam_y, screening)
+    block1, sibling0, own0, matrix_y, matrix_z, weights = lax.optimization_barrier(
+        (block1, sibling0, own0, matrix_y, matrix_z, weights)
     )
     token = send(sibling0[:8, :LANES], 1, (0,))
     block2, block3, token = lax.optimization_barrier((block2, block3, token))
@@ -343,7 +362,7 @@
     along = forward_y(1, block1, (own0, own1), matrix_y, token, None)
     along = forward_y(0, block0, (sibling0, sibling1), matrix_y, token, along)
     columns = lax.all_to_all(along.reshape(32, 64, TILE), WIDE, 0, 0, tiled=True)
-    back = solve_z(columns, matrix_z, lam_z, lam_y, screening)
+    back = solve_z(columns, matrix_z, weights)
     rows = lax.all_to_all(back, WIDE, 0, 0, tiled=True).reshape(4, 8, 64, TILE)
     block1, block2 = backward_y(1, rows, matrix_y)
     block0, block3 = backward_y(0, rows, matrix_y)

time: 134 us -> 133 us (level)
  waiting for transfers between devices: 30.7 us -> 25 us
  starting transfers between devices: 20.1 us -> 24.6 us
  Pallas kernels: 29.8 us -> 27.2 us
  local copies, waits for them, and re-layouts: 0.04 us -> 1.74 us
  blocking collectives: 52.3 us -> 53.8 us
    ppermute x11, waiting for transfers between devices: 30.7 us -> 25 us  [send(): lax.ppermute(block, NARROW, [(n, n ^ d) for n in range(4) if n % 2 in cor...]
    ppermute x11, starting transfers between devices: 20.1 us -> 24.6 us  [send(): lax.ppermute(block, NARROW, [(n, n ^ d) for n in range(4) if n % 2 in cor...]
    pallas_call x1 -> x2, Pallas kernels: 11.4 us -> 9.22 us  [the longest x1 8.18 us: solve_z(): call(solve_z_kernel, 'solve_z', [VMEM] * 6, VMEM, jax.ShapeDtypeStruct((3...]
    unnamed x14, local copies, waits for them, and re-layouts: 0.04 us -> 1.74 us
    all_to_all x1, blocking collectives: 30.8 us -> 32.3 us  [on_device(): lax.all_to_all(along.reshape(32, 64, TILE), WIDE, 0, 0, tiled=True)]
  transfers between devices with their start and end apart: 11 -> 11, of which waited for: 6 -> 6; matrix products, arithmetic and copies ran while one was open for 0% -> 0% of each run, Pallas kernels for 8% -> 9%
where the time goes in v5:
time: 133 us
  blocking collectives  53.8 us (40%)
  Pallas kernels  27.2 us (20%)
  waiting for transfers between devices  25 us (19%)
  starting transfers between devices  24.6 us (18%)
  local copies, waits for them, and re-layouts  1.74 us (1%)
    all_to_all x1, blocking collectives, on_device(): lax.all_to_all(along.reshape(32, 64, TILE), WIDE, 0, 0, tiled=True)  32.3 us
    ppermute x11, waiting for transfers between devices, send(): lax.ppermute(block, NARROW, [(n, n ^ d) for n in range(4) if n % 2 in cor...  25 us
    ppermute x11, starting transfers between devices, send(): lax.ppermute(block, NARROW, [(n, n ^ d) for n in range(4) if n % 2 in cor...  24.6 us
    all_to_all x1, blocking collectives, on_device(): rows = lax.all_to_all(back, WIDE, 0, 0, tiled=True).reshape(4, 8, 64, TILE)  21.6 us
    pallas_call x1, Pallas kernels, solve_z(): call(solve_z_kernel, 'solve_z', [VMEM] * 6, VMEM, jax.ShapeDtypeStruct((3...  8.18 us
    pallas_call x2, Pallas kernels, backward_y(): call(kernel, 'backward_y', [VMEM] * 5, [VMEM] * 2, [jax.ShapeDtypeStruct(...  4.79 us
    pallas_call x2, Pallas kernels, forward_y(): call(kernel, 'forward_y', [VMEM] * (8 + len(more)), VMEM, jax.ShapeDtypeS...  4.21 us
    pallas_call x2, Pallas kernels, make_source(): call(kernel, 'make_source', [HBM] * 2, [VMEM] * count, [jax.ShapeDtypeStr...  3.53 us
  transfers between devices with their start and end apart: 11, of which 6 were waited for; matrix products, arithmetic and copies ran while one was open for 0% of the time, Pallas kernels for 9%

profile of v5, /device:TPU:1, one launch (start us, length us, event | category | flops | bytes accessed | tf_op | source)
XLA Modules:
  0.0 132.8 jit_solution(1109139869677694084)
XLA Ops:
  0.0 1.8 %make_source.2 = (f32[256,512]{1,0:T(8,128)S(1)}, f32[256,512]{1,0:T(8,128)S(1)}) custom-call(f32[16,64,512]{2,1,0:T(8,128)} %refs_0_.5, s32[16,64,512]{2,1,0:T(8,128)} %refs_1_.5), custom_call_target="tpu_custom_call" | custom-call | flops 1048576 | bytes 10485760 | tf_op jit(solution)/shard_map/make_source/pallas_call | solution.py:108
  1.8 1.5 %collective-permute-start = (f32[256,512]{1,0:T(8,128)S(1)}, f32[256,512]{1,0:T(8,128)S(1)}, u32[]{:S(2)}, u32[]{:S(2)}) collective-permute-start(f32[256,512]{1,0:T(8,128)S(1)} %get-tuple-element.41), channel_id=1, source_target_pairs={{0,32},{32,0},{64,96},{96,64},{1,33},{33,1},{65,97},{97,65},{2,34}... | collective-permute-start | bytes 1572872 | tf_op jit(solution)/shard_map/ppermute | solution.py:158
  4.1 1.8 %make_source.3 = (f32[256,512]{1,0:T(8,128)S(1)}, f32[256,512]{1,0:T(8,128)S(1)}) custom-call(f32[16,64,512]{2,1,0:T(8,128)} %refs_0_.5, s32[16,64,512]{2,1,0:T(8,128)} %refs_1_.5), custom_call_target="tpu_custom_call" | custom-call | flops 1048576 | bytes 10485760 | tf_op jit(solution)/shard_map/make_source/pallas_call | solution.py:108
  5.9 4.6 %collective-permute-start.1 = (f32[256,512]{1,0:T(8,128)S(1)}, f32[256,512]{1,0:T(8,128)S(1)}, u32[]{:S(2)}, u32[]{:S(2)}) collective-permute-start(f32[256,512]{1,0:T(8,128)S(1)} %get-tuple-element.45), channel_id=1, source_target_pairs={{0,32},{32,0},{64,96},{96,64},{1,33},{33,1},{65,97},{97,65},{2,34}... | collective-permute-start | bytes 1572872 | tf_op jit(solution)/shard_map/ppermute | solution.py:158
  12.3 1.7 %prepare.2 = (bf16[1024,1024]{1,0:T(8,128)(2,1)S(1)}, bf16[1024,1024]{1,0:T(8,128)(2,1)S(1)}, bf16[1024,1024]{1,0:T(8,128)(2,1)S(1)}, bf16[1024,1024]{1,0:T(8,128)(2,1)S(1)}) custom-call(f32[1024,1024]{1,0:T(8,128)S(1)} %copy-done, f32[1024,1024]{1,0:T(8,128)S(1)} %copy-done.1), custom_call_target="tpu_custom_call" | custom-call | flops 2147483648 | bytes 10485760 | tf_op jit(solution)/shard_map/prepare/pallas_call | solution.py:145
  14.5 1.3 copy-done.3
  15.8 1.7 %prepare.3 = (bf16[1024,1024]{1,0:T(8,128)(2,1)S(1)}, bf16[1024,1024]{1,0:T(8,128)(2,1)S(1)}, bf16[1024,1024]{1,0:T(8,128)(2,1)S(1)}, bf16[1024,1024]{1,0:T(8,128)(2,1)S(1)}) custom-call(f32[1024,1024]{1,0:T(8,128)S(1)} %copy-done.2, f32[1024,1024]{1,0:T(8,128)S(1)} %copy-done.3), custom_call_target="tpu_custom_call" | custom-call | flops 2147483648 | bytes 10485760 | tf_op jit(solution)/shard_map/prepare/pallas_call | solution.py:145
  17.6 1.3 collective-permute-start.4
  18.9 6.2 %collective-permute-done.4.refs_7_ = f32[8,128]{1,0:T(8,128)S(1)} collective-permute-done((f32[8,128]{1,0:T(8,128)S(1)}, f32[8,128]{1,0:T(8,128)S(1)}, u32[]{:S(2)}, u32[]{:S(2)}) %collective-permute-start.4) | collective-permute-done | bytes 4128 | tf_op jit(solution)/shard_map/ppermute | solution.py:158
  25.0 3.4 %collective-permute-start.6 = (f32[256,512]{1,0:T(8,128)S(1)}, f32[256,512]{1,0:T(8,128)S(1)}, u32[]{:S(2)}, u32[]{:S(2)}) collective-permute-start(f32[256,512]{1,0:T(8,128)S(1)} %get-tuple-element.65), channel_id=1, source_target_pairs={{32,96},{96,32},{33,97},{97,33},{34,98},{98,34},{35,99},{99,35},{3... | collective-permute-start | bytes 1572872 | tf_op jit(solution)/shard_map/ppermute | solution.py:158
  28.5 3.4 %collective-permute-start.5 = (f32[256,512]{1,0:T(8,128)S(1)}, f32[256,512]{1,0:T(8,128)S(1)}, u32[]{:S(2)}, u32[]{:S(2)}) collective-permute-start(f32[256,512]{1,0:T(8,128)S(1)} %collective-permute-done), channel_id=1, source_target_pairs={{32,96},{96,32},{33,97},{97,33},{34,98},{98,34},{35,99},{99,35},{3... | collective-permute-start | bytes 1572872 | tf_op jit(solution)/shard_map/ppermute | solution.py:158
  31.8 4.6 %collective-permute-done.6.refs_2_ = f32[256,512]{1,0:T(8,128)S(1)} collective-permute-done((f32[256,512]{1,0:T(8,128)S(1)}, f32[256,512]{1,0:T(8,128)S(1)}, u32[]{:S(2)}, u32[]{:S(2)}) %collective-permute-start.6) | collective-permute-done | bytes 524320 | tf_op jit(solution)/shard_map/ppermute | solution.py:158
  36.5 2.1 %forward_y.2.refs_8_ = f32[4,8,64,256]{3,2,1,0:T(8,128)S(1)} custom-call(f32[256,512]{1,0:T(8,128)S(1)} %collective-permute-done.1.refs_0_, f32[256,512]{1,0:T(8,128)S(1)} %collective-permute-done.3.refs_1_, f32[256,512]{1,0:T(8,128)S(1)} %collective-permute-done.6.refs_2_, bf16[1024,1024]{1,0:T(8,128)(2,1)S(1)} %get-tuple-element.58.refs_3_.refs_1_, ...), custom_call_target="tpu_custom_call" | custom-call | flops 2147483648 | bytes 10485760 | tf_op jit(solution)/shard_map/forward_y/pallas_call | solution.py:195
  38.6 3.5 %collective-permute-done.5.refs_2_ = f32[256,512]{1,0:T(8,128)S(1)} collective-permute-done((f32[256,512]{1,0:T(8,128)S(1)}, f32[256,512]{1,0:T(8,128)S(1)}, u32[]{:S(2)}, u32[]{:S(2)}) %collective-permute-start.5) | collective-permute-done | bytes 524320 | tf_op jit(solution)/shard_map/ppermute | solution.py:158
  42.1 2.1 %forward_y.3 = f32[4,8,64,256]{3,2,1,0:T(8,128)S(1)} custom-call(f32[256,512]{1,0:T(8,128)S(1)} %get-tuple-element.44.refs_0_, f32[256,512]{1,0:T(8,128)S(1)} %collective-permute-done.2.refs_1_, f32[256,512]{1,0:T(8,128)S(1)} %collective-permute-done.5.refs_2_, bf16[1024,1024]{1,0:T(8,128)(2,1)S(1)} %get-tuple-element.58.refs_3_.refs_1_, ...), custom_call_target="tpu_custom_call" | custom-call | flops 2147483648 | bytes 10485760 | tf_op jit(solution)/shard_map/forward_y/pallas_call | solution.py:195
  44.2 32.3 %all_to_all.10.x_ref = f32[32,64,256]{2,1,0:T(8,128)S(1)} all-to-all(f32[32,64,256]{2,1,0:T(8,128)S(1)} %bitcast.7), channel_id=1, replica_groups=mesh['yh'=2,'core'=2,'z'=4,'yl'=2,'x'=4] {'z','yl','x'}, dimensions={0} | all-to-all | bytes 4194304 | tf_op jit(solution)/shard_map/all_to_all | solution.py:364
  76.5 8.2 %solve_z.1 = f32[32,64,256]{2,1,0:T(8,128)S(1)} custom-call(f32[32,64,256]{2,1,0:T(8,128)S(1)} %all_to_all.10.x_ref, bf16[1024,1024]{1,0:T(8,128)(2,1)S(1)} %get-tuple-element.66.eh, bf16[1024,1024]{1,0:T(8,128)(2,1)S(1)} %get-tuple-element.67.el, bf16[1024,1024]{1,0:T(8,128)(2,1)S(1)} %get-tuple-element.68.oh, bf16[1024,1024]{1,0:T(8,128)(2,1)S(1)} %get-tuple-element.69.ol, ...), custom_call_target="tpu_custom_call" | custom-call | flops 6442450944 | bytes 10485760 | tf_op jit(solution)/shard_map/solve_z/pallas_call | solution.py:266
  84.7 21.6 %all_to_all.11 = f32[32,64,256]{2,1,0:T(8,128)S(1)} all-to-all(f32[32,64,256]{2,1,0:T(8,128)S(1)} %solve_z.1), channel_id=1, replica_groups=mesh['yh'=2,'core'=2,'z'=4,'yl'=2,'x'=4] {'z','yl','x'}, dimensions={0} | all-to-all | bytes 4194304 | tf_op jit(solution)/shard_map/all_to_all | solution.py:366
  106.2 2.4 %backward_y.3 = (f32[256,512]{1,0:T(8,128)S(1)}, f32[256,512]{1,0:T(8,128)S(1)}) custom-call(f32[4,8,64,256]{3,2,1,0:T(8,128)S(1)} %bitcast.5, bf16[1024,1024]{1,0:T(8,128)(2,1)S(1)} %get-tuple-element.58.refs_3_.refs_1_, bf16[1024,1024]{1,0:T(8,128)(2,1)S(1)} %get-tuple-element.59.refs_4_.refs_2_, bf16[1024,1024]{1,0:T(8,128)(2,1)S(1)} %get-tuple-element.60.refs_5_.refs_3_, ...), custom_call_target="tpu_custom_call" | custom-call | flops 2147483648 | bytes 10485760 | tf_op jit(solution)/shard_map/backward_y/pallas_call | solution.py:301
  108.6 8.8 %collective-permute-start.9 = (f32[256,512]{1,0:T(8,128)S(1)}, f32[256,512]{1,0:T(8,128)S(1)}, u32[]{:S(2)}, u32[]{:S(2)}) collective-permute-start(f32[256,512]{1,0:T(8,128)S(1)} %get-tuple-element.74), channel_id=1, source_target_pairs={{0,64},{32,96},{64,0},{96,32},{1,65},{33,97},{65,1},{97,33},{2,66}... | collective-permute-start | bytes 1572872 | tf_op jit(solution)/shard_map/ppermute | solution.py:158
  117.4 2.4 %backward_y.2 = (f32[256,512]{1,0:T(8,128)S(1)}, f32[256,512]{1,0:T(8,128)S(1)}) custom-call(f32[4,8,64,256]{3,2,1,0:T(8,128)S(1)} %bitcast.6, bf16[1024,1024]{1,0:T(8,128)(2,1)S(1)} %get-tuple-element.58.refs_3_.refs_1_, bf16[1024,1024]{1,0:T(8,128)(2,1)S(1)} %get-tuple-element.59.refs_4_.refs_2_, bf16[1024,1024]{1,0:T(8,128)(2,1)S(1)} %get-tuple-element.60.refs_5_.refs_3_, ...), custom_call_target="tpu_custom_call" | custom-call | flops 2147483648 | bytes 10485760 | tf_op jit(solution)/shard_map/backward_y/pallas_call | solution.py:301
  119.9 4.4 %collective-permute-done.9.refs_2_ = f32[256,512]{1,0:T(8,128)S(1)} collective-permute-done((f32[256,512]{1,0:T(8,128)S(1)}, f32[256,512]{1,0:T(8,128)S(1)}, u32[]{:S(2)}, u32[]{:S(2)}) %collective-permute-start.9) | collective-permute-done | bytes 524320 | tf_op jit(solution)/shard_map/ppermute | solution.py:158
  124.3 5.6 %collective-permute-done.7 = f32[256,512]{1,0:T(8,128)S(1)} collective-permute-done((f32[256,512]{1,0:T(8,128)S(1)}, f32[256,512]{1,0:T(8,128)S(1)}, u32[]{:S(2)}, u32[]{:S(2)}) %collective-permute-start.7) | collective-permute-done | bytes 524320 | tf_op jit(solution)/shard_map/ppermute | solution.py:158
  129.9 1.2 place.2.refs_1_
  (27 shorter events, 4.6 us)
Async XLA Ops:
  0.0 12.3 %copy-start.1 = (f32[1024,1024]{1,0:T(8,128)S(1)}, f32[1024,1024]{1,0:T(8,128)}, u32[]{:S(2)}) copy-start(f32[1024,1024]{1,0:T(8,128)} %refs_1_.6) | copy-start | bytes 12582916
  1.8 4.1 %collective-permute-start = (f32[256,512]{1,0:T(8,128)S(1)}, f32[256,512]{1,0:T(8,128)S(1)}, u32[]{:S(2)}, u32[]{:S(2)}) collective-permute-start(f32[256,512]{1,0:T(8,128)S(1)} %get-tuple-element.41), channel_id=1, source_target_pairs={{0,32},{32,0},{64,96},{96,64},{1,33},{33,1},{65,97},{97,65},{2,34}... | collective-permute-start | bytes 1572872 | tf_op jit(solution)/shard_map/ppermute | solution.py:158
  3.3 7.9 %copy-start.4 = (f32[2048]{0:T(1024)S(1)}, f32[2048]{0:T(1024)}, u32[]{:S(2)}) copy-start(f32[2048]{0:T(1024)} %param.17) | copy-start | bytes 24580
  3.3 8.0 %copy-start.5 = (f32[2048]{0:T(1024)S(1)}, f32[2048]{0:T(1024)}, u32[]{:S(2)}) copy-start(f32[2048]{0:T(1024)} %param.16) | copy-start | bytes 24580
  3.3 8.0 %copy-start.6 = (f32[16]{0:T(128)S(1)}, f32[16]{0:T(128)}, u32[]{:S(2)}) copy-start(f32[16]{0:T(128)} %screen_ref.1) | copy-start | bytes 196
  3.3 14.2 %collective-permute-start.3 = (f32[256,512]{1,0:T(8,128)S(1)}, f32[256,512]{1,0:T(8,128)S(1)}, u32[]{:S(2)}, u32[]{:S(2)}) collective-permute-start(f32[256,512]{1,0:T(8,128)S(1)} %get-tuple-element.65), channel_id=1, source_target_pairs={{0,64},{64,0},{1,65},{65,1},{2,66},{66,2},{3,67},{67,3},{4,68},{68... | collective-permute-start | bytes 1572872 | tf_op jit(solution)/shard_map/ppermute | solution.py:158
  4.1 8.2 %copy-start = (f32[1024,1024]{1,0:T(8,128)S(1)}, f32[1024,1024]{1,0:T(8,128)}, u32[]{:S(2)}) copy-start(f32[1024,1024]{1,0:T(8,128)} %refs_0_.6) | copy-start | bytes 12582916
  5.9 11.6 %collective-permute-start.1 = (f32[256,512]{1,0:T(8,128)S(1)}, f32[256,512]{1,0:T(8,128)S(1)}, u32[]{:S(2)}, u32[]{:S(2)}) collective-permute-start(f32[256,512]{1,0:T(8,128)S(1)} %get-tuple-element.45), channel_id=1, source_target_pairs={{0,32},{32,0},{64,96},{96,64},{1,33},{33,1},{65,97},{97,65},{2,34}... | collective-permute-start | bytes 1572872 | tf_op jit(solution)/shard_map/ppermute | solution.py:158
  10.5 7.0 %collective-permute-start.2 = (f32[256,512]{1,0:T(8,128)S(1)}, f32[256,512]{1,0:T(8,128)S(1)}, u32[]{:S(2)}, u32[]{:S(2)}) collective-permute-start(f32[256,512]{1,0:T(8,128)S(1)} %collective-permute-done), channel_id=1, source_target_pairs={{0,64},{64,0},{1,65},{65,1},{2,66},{66,2},{3,67},{67,3},{4,68},{68... | collective-permute-start | bytes 1572872 | tf_op jit(solution)/shard_map/ppermute | solution.py:158
  12.3 2.2 %copy-start.2 = (f32[1024,1024]{1,0:T(8,128)S(1)}, f32[1024,1024]{1,0:T(8,128)}, u32[]{:S(2)}) copy-start(f32[1024,1024]{1,0:T(8,128)} %refs_0_.7) | copy-start | bytes 12582916
  12.3 3.5 %copy-start.3 = (f32[1024,1024]{1,0:T(8,128)S(1)}, f32[1024,1024]{1,0:T(8,128)}, u32[]{:S(2)}) copy-start(f32[1024,1024]{1,0:T(8,128)} %refs_1_.7) | copy-start | bytes 12582916
  17.6 7.5 %collective-permute-start.4 = (f32[8,128]{1,0:T(8,128)S(1)}, f32[8,128]{1,0:T(8,128)S(1)}, u32[]{:S(2)}, u32[]{:S(2)}) collective-permute-start(f32[8,128]{1,0:T(8,128)S(1)} %slice.3), channel_id=1, source_target_pairs={{0,32},{64,96},{1,33},{65,97},{2,34},{66,98},{3,35},{67,99},{4,36}... | collective-permute-start | bytes 12296 | tf_op jit(solution)/shard_map/ppermute | solution.py:158
  25.0 11.4 %collective-permute-start.6 = (f32[256,512]{1,0:T(8,128)S(1)}, f32[256,512]{1,0:T(8,128)S(1)}, u32[]{:S(2)}, u32[]{:S(2)}) collective-permute-start(f32[256,512]{1,0:T(8,128)S(1)} %get-tuple-element.65), channel_id=1, source_target_pairs={{32,96},{96,32},{33,97},{97,33},{34,98},{98,34},{35,99},{99,35},{3... | collective-permute-start | bytes 1572872 | tf_op jit(solution)/shard_map/ppermute | solution.py:158
  28.5 13.6 %collective-permute-start.5 = (f32[256,512]{1,0:T(8,128)S(1)}, f32[256,512]{1,0:T(8,128)S(1)}, u32[]{:S(2)}, u32[]{:S(2)}) collective-permute-start(f32[256,512]{1,0:T(8,128)S(1)} %collective-permute-done), channel_id=1, source_target_pairs={{32,96},{96,32},{33,97},{97,33},{34,98},{98,34},{35,99},{99,35},{3... | collective-permute-start | bytes 1572872 | tf_op jit(solution)/shard_map/ppermute | solution.py:158
  108.6 15.6 %collective-permute-start.9 = (f32[256,512]{1,0:T(8,128)S(1)}, f32[256,512]{1,0:T(8,128)S(1)}, u32[]{:S(2)}, u32[]{:S(2)}) collective-permute-start(f32[256,512]{1,0:T(8,128)S(1)} %get-tuple-element.74), channel_id=1, source_target_pairs={{0,64},{32,96},{64,0},{96,32},{1,65},{33,97},{65,1},{97,33},{2,66}... | collective-permute-start | bytes 1572872 | tf_op jit(solution)/shard_map/ppermute | solution.py:158
  119.8 10.1 %collective-permute-start.7 = (f32[256,512]{1,0:T(8,128)S(1)}, f32[256,512]{1,0:T(8,128)S(1)}, u32[]{:S(2)}, u32[]{:S(2)}) collective-permute-start(f32[256,512]{1,0:T(8,128)S(1)} %get-tuple-element.71), channel_id=1, source_target_pairs={{0,64},{32,96},{64,0},{96,32},{1,65},{33,97},{65,1},{97,33},{2,66}... | collective-permute-start | bytes 1572872 | tf_op jit(solution)/shard_map/ppermute | solution.py:158
  124.3 5.6 %collective-permute-start.10 = (f32[256,512]{1,0:T(8,128)S(1)}, f32[256,512]{1,0:T(8,128)S(1)}, u32[]{:S(2)}, u32[]{:S(2)}) collective-permute-start(f32[256,512]{1,0:T(8,128)S(1)} %get-tuple-element.75), channel_id=1, source_target_pairs={{0,32},{32,0},{64,96},{96,64},{1,33},{33,1},{65,97},{97,65},{2,34}... | collective-permute-start | bytes 1572872 | tf_op jit(solution)/shard_map/ppermute | solution.py:158
  129.9 1.9 %collective-permute-start.8 = (f32[256,512]{1,0:T(8,128)S(1)}, f32[256,512]{1,0:T(8,128)S(1)}, u32[]{:S(2)}, u32[]{:S(2)}) collective-permute-start(f32[256,512]{1,0:T(8,128)S(1)} %collective-permute-done.7), channel_id=1, source_target_pairs={{0,32},{32,0},{64,96},{96,64},{1,33},{33,1},{65,97},{97,65},{2,34}... | collective-permute-start | bytes 1572872 | tf_op jit(solution)/shard_map/ppermute | solution.py:158
